TPU v7x, 32 devices: a whole 2x2x4 slice. The times are simulated.
32 devices in a mesh: dp: 8 (over y, x, core), tensor: 4 (over z).
Axes of the slice: x: 2, y: 2, z: 4, core: 2. Of those that a mesh axis runs over, the one named last changes fastest.
Arguments:
- block_input: bfloat16 [8192, 2560], P(('dp', 'tensor')), may hold values from -6 to 6
- segment_ids: int32 [8, 1024], P('dp'), may hold values from 0 to 2, never falling along the last dimension, each value on 1 to 512 neighbouring positions
- output_cotangent: bfloat16 [8192, 2560], P(('dp', 'tensor')), may hold values from -6 to 6
- first_gain: bfloat16 [2560], replicated, may hold values from 0.25 to 1.75
- input_weight: bfloat16 [2560, 2560], P('dp', 'tensor'), may hold values from -0.125 to 0.125
- gelu_weight: bfloat16 [2560, 2560], P('dp', 'tensor'), may hold values from -0.125 to 0.125
- conv_kernel: bfloat16 [4, 2560], P(None, 'tensor'), may hold values from -3 to 3
- conv_bias: bfloat16 [2560], P('tensor'), may hold values from -3 to 3
- alpha_weight: bfloat16 [8, 320, 320], P('tensor'), may hold values from -0.3125 to 0.3125
- alpha_bias: bfloat16 [2560], P('tensor'), may hold values from -4 to 4
- update_weight: bfloat16 [8, 320, 320], P('tensor'), may hold values from -0.3125 to 0.3125
- update_bias: bfloat16 [2560], P('tensor'), may hold values from -4 to 4
- decay_param: bfloat16 [2560], P('tensor'), may hold values from -9 to -1
- mixer_weight: bfloat16 [2560, 2560], P('tensor', 'dp'), may hold values from -0.125 to 0.125
- second_gain: bfloat16 [2560], replicated, may hold values from 0.25 to 1.75
- gate_weight: bfloat16 [2560, 7680], P('dp', 'tensor'), may hold values from -0.125 to 0.125
- up_weight: bfloat16 [2560, 7680], P('dp', 'tensor'), may hold values from -0.125 to 0.125
- down_weight: bfloat16 [7680, 2560], P('tensor', 'dp'), may hold values from -0.0625 to 0.0625
Outputs:
- block_output: bfloat16 [8192, 2560], P(('dp', 'tensor'))
- input_grad: float32 [8192, 2560], P(('dp', 'tensor'))
- grad_first_gain: float32 [2560], replicated
- grad_input_weight: float32 [2560, 2560], P('dp', 'tensor')
- grad_gelu_weight: float32 [2560, 2560], P('dp', 'tensor')
- grad_conv_kernel: float32 [4, 2560], P(None, 'tensor')
- grad_conv_bias: float32 [2560], P('tensor')
- grad_alpha_weight: float32 [8, 320, 320], P('tensor')
- grad_alpha_bias: float32 [2560], P('tensor')
- grad_update_weight: float32 [8, 320, 320], P('tensor')
- grad_update_bias: float32 [2560], P('tensor')
- grad_decay_param: float32 [2560], P('tensor')
- grad_mixer_weight: float32 [2560, 2560], P('tensor', 'dp')
- grad_second_gain: float32 [2560], replicated
- grad_gate_weight: float32 [2560, 7680], P('dp', 'tensor')
- grad_up_weight: float32 [2560, 7680], P('dp', 'tensor')
- grad_down_weight: float32 [7680, 2560], P('tensor', 'dp')
Inputs may be any that keep to these rules, and one draw needn't show every extreme that they name: `segment_ids`: along each sequence of 1024 tokens the numbers never fall; a document starts at the first token and wherever the number changes; a document has at most 512 tokens.
All inputs are finite; a program needn't handle non-finite values.
Results may differ from a plain program's by a relative error of at most 0.0087.
Values may be sent and summed in bfloat16 or wider, within the bound.
A program may use at most 320 MiB of HBM per device.

v0:
```python
from functools import partial

import jax
import jax.numpy as jnp
from jax import lax
from jax.sharding import PartitionSpec as P

EPSILON = 1e-06
RATE_SCALE = 8.0


def norm_rows(values, gain):
    inverse = lax.rsqrt(jnp.mean(values * values, axis=-1, keepdims=True) + EPSILON)
    return values * inverse * gain


def delayed(values, offset):
    filler = jnp.zeros_like(values[:, :offset])
    return jnp.concatenate([filler, values[:, : values.shape[1] - offset]], axis=1)


def document_masks(segment_ids, kernel_size):
    masks = [None]
    for offset in range(1, kernel_size):
        filler = jnp.full((segment_ids.shape[0], offset), -1, jnp.int32)
        earlier = jnp.concatenate([filler, segment_ids[:, : segment_ids.shape[1] - offset]], axis=1)
        masks.append((earlier == segment_ids).astype(jnp.float32)[:, :, None])
    return masks


def conv_local(masks, branch, kernel, bias):
    summed = branch * kernel[0] + bias
    for offset in range(1, kernel.shape[0]):
        summed = summed + delayed(branch, offset) * masks[offset] * kernel[offset]
    return summed


def recurrence_inputs(keeping, conv_out, alpha_pre, update_pre, decay_param):
    alpha_gate = jax.nn.sigmoid(alpha_pre)
    update_gate = jax.nn.sigmoid(update_pre)
    log_decay = -RATE_SCALE * alpha_gate * jax.nn.softplus(decay_param)
    scaling = keeping * jnp.sqrt(-jnp.expm1(2.0 * log_decay)) + (1.0 - keeping)
    return (keeping * jnp.exp(log_decay), conv_out * update_gate * scaling)


def linked(earlier, later):
    return (earlier[0] * later[0], later[0] * earlier[1] + later[1])


def gated_hidden(gate_vals, up_vals):
    return jax.nn.gelu(gate_vals, approximate=True) * up_vals


def gelu_tanh(values):
    return jax.nn.gelu(values, approximate=True)


def matmul(left, right):
    return jnp.dot(left, right, preferred_element_type=jnp.float32)


def inner_rows(left, right):
    return lax.dot_general(
        left, right, (((0,), (0,)), ((), ())), preferred_element_type=jnp.float32
    )


def times_transposed(left, right):
    return lax.dot_general(
        left, right, (((1,), (1,)), ((), ())), preferred_element_type=jnp.float32
    )


def body(
    block_input,
    segment_ids,
    output_cotangent,
    first_gain,
    input_weight,
    gelu_weight,
    conv_kernel,
    conv_bias,
    alpha_weight,
    alpha_bias,
    update_weight,
    update_bias,
    decay_param,
    mixer_weight,
    second_gain,
    gate_weight,
    up_weight,
    down_weight,
):
    gathered = (
        lax.all_gather(input_weight, "dp", axis=0, tiled=True),
        lax.all_gather(gelu_weight, "dp", axis=0, tiled=True),
        lax.all_gather(mixer_weight, "dp", axis=1, tiled=True),
        lax.all_gather(gate_weight, "dp", axis=0, tiled=True),
        lax.all_gather(up_weight, "dp", axis=0, tiled=True),
        lax.all_gather(down_weight, "dp", axis=1, tiled=True),
    )
    input_all, gelu_all, mixer_all, gate_all, upward_all, down_all = gathered
    seq_count, length = segment_ids.shape
    token_count = seq_count * length
    rows_own = block_input.shape[0]
    position = lax.axis_index("tensor") * rows_own
    channels = input_weight.shape[1]
    blocks = alpha_weight.shape[0]
    block_width = alpha_weight.shape[1]
    gain_one = first_gain.astype(jnp.float32)
    gain_two = second_gain.astype(jnp.float32)
    kernel_f = conv_kernel.astype(jnp.float32)
    bias_f = conv_bias.astype(jnp.float32)
    decay_f = decay_param.astype(jnp.float32)
    masks = document_masks(segment_ids, conv_kernel.shape[0])
    keeping = masks[1]
    inputs_f = block_input.astype(jnp.float32)
    normed = norm_rows(inputs_f, gain_one).astype(jnp.bfloat16)
    normed_all = lax.all_gather(normed, "tensor", axis=0, tiled=True)
    branch = matmul(normed_all, input_all).reshape(seq_count, length, channels)
    gate_pre = matmul(normed_all, gelu_all)
    gelu_out, gelu_back = jax.vjp(gelu_tanh, gate_pre)
    conv_fn = partial(conv_local, masks)
    conv_sum, conv_back = jax.vjp(conv_fn, branch, kernel_f, bias_f)
    conv_low = conv_sum.astype(jnp.bfloat16)
    grouped = conv_low.reshape(token_count, blocks, block_width)
    alpha_pre = jnp.einsum(
        "tbi,bij->tbj", grouped, alpha_weight, preferred_element_type=jnp.float32
    ).reshape(seq_count, length, channels) + alpha_bias.astype(jnp.float32)
    update_pre = jnp.einsum(
        "tbi,bij->tbj", grouped, update_weight, preferred_element_type=jnp.float32
    ).reshape(seq_count, length, channels) + update_bias.astype(jnp.float32)
    recur_fn = partial(recurrence_inputs, keeping)
    (decay, driven), recur_back = jax.vjp(
        recur_fn, conv_low.astype(jnp.float32), alpha_pre, update_pre, decay_f
    )
    states = lax.associative_scan(linked, (decay, driven), axis=1)[1]
    state_rows = states.reshape(token_count, channels)
    mixed = (state_rows * gelu_out).astype(jnp.bfloat16)
    mix_terms = matmul(mixed, mixer_all)
    own_terms = lax.dynamic_slice_in_dim(mix_terms, position, rows_own, 0) + inputs_f
    placed = lax.dynamic_update_slice_in_dim(mix_terms, own_terms, position, 0)
    middle_all = lax.psum(placed, "tensor")
    second_all = norm_rows(middle_all, gain_two).astype(jnp.bfloat16)
    middle = lax.dynamic_slice_in_dim(middle_all, position, rows_own, 0)
    gate_vals = matmul(second_all, gate_all)
    up_vals = matmul(second_all, upward_all)
    hidden, hidden_back = jax.vjp(gated_hidden, gate_vals, up_vals)
    hidden_low = hidden.astype(jnp.bfloat16)
    middle_out = middle + lax.psum_scatter(
        matmul(hidden_low, down_all), "tensor", scatter_dimension=0, tiled=True
    )
    block_output = middle_out.astype(jnp.bfloat16)
    cotangent_all = lax.all_gather(output_cotangent, "tensor", axis=0, tiled=True)
    grad_down = inner_rows(hidden_low, cotangent_all)
    d_hidden = times_transposed(cotangent_all, down_all)
    d_gate, d_up = hidden_back(d_hidden)
    d_gate_low = d_gate.astype(jnp.bfloat16)
    d_up_low = d_up.astype(jnp.bfloat16)
    grad_gate = inner_rows(second_all, d_gate_low)
    grad_upward = inner_rows(second_all, d_up_low)
    second_terms = times_transposed(d_gate_low, gate_all) + times_transposed(d_up_low, upward_all)
    d_second_all = lax.psum(second_terms, "tensor")
    _, full_back = jax.vjp(partial(norm_rows, gain=gain_two), middle_all)
    d_middle_full = cotangent_all.astype(jnp.float32) + full_back(d_second_all)[0]
    d_middle_all = d_middle_full.astype(jnp.bfloat16)
    d_middle = lax.dynamic_slice_in_dim(d_middle_full, position, rows_own, 0)
    own_second = lax.dynamic_slice_in_dim(d_second_all, position, rows_own, 0)
    own_inverse = lax.rsqrt(jnp.mean(middle * middle, axis=-1, keepdims=True) + EPSILON)
    grad_gain_two = jnp.sum(own_second * middle * own_inverse, axis=0)
    grad_mixer = inner_rows(mixed, d_middle_all)
    d_mixed = times_transposed(d_middle_all, mixer_all)
    d_states = (d_mixed * gelu_out).reshape(seq_count, length, channels)
    d_gate_pre = gelu_back(d_mixed * state_rows)[0].astype(jnp.bfloat16)
    decay_next = jnp.concatenate([decay[:, 1:], jnp.zeros_like(decay[:, :1])], axis=1)
    adjoint = lax.associative_scan(linked, (decay_next, d_states), reverse=True, axis=1)[1]
    d_decay = adjoint * delayed(states, 1)
    d_conv_direct, d_alpha_pre, d_update_pre, grad_decay = recur_back((d_decay, adjoint))
    alpha_low = d_alpha_pre.astype(jnp.bfloat16).reshape(token_count, blocks, block_width)
    update_low = d_update_pre.astype(jnp.bfloat16).reshape(token_count, blocks, block_width)
    grad_alpha = jnp.einsum("tbi,tbj->bij", grouped, alpha_low, preferred_element_type=jnp.float32)
    grad_update = jnp.einsum(
        "tbi,tbj->bij", grouped, update_low, preferred_element_type=jnp.float32
    )
    grad_alpha_bias = jnp.sum(alpha_low.astype(jnp.float32), axis=0).reshape(channels)
    grad_update_bias = jnp.sum(update_low.astype(jnp.float32), axis=0).reshape(channels)
    through_gates = jnp.einsum(
        "tbj,bij->tbi", alpha_low, alpha_weight, preferred_element_type=jnp.float32
    ) + jnp.einsum("tbj,bij->tbi", update_low, update_weight, preferred_element_type=jnp.float32)
    d_conv = d_conv_direct + through_gates.reshape(seq_count, length, channels)
    d_branch, grad_kernel, grad_bias = conv_back(d_conv)
    d_branch_low = d_branch.reshape(token_count, channels).astype(jnp.bfloat16)
    grad_input = inner_rows(normed_all, d_branch_low)
    grad_gelu = inner_rows(normed_all, d_gate_pre)
    d_normed = lax.psum_scatter(
        times_transposed(d_branch_low, input_all) + times_transposed(d_gate_pre, gelu_all),
        "tensor",
        scatter_dimension=0,
        tiled=True,
    )
    _, norm_one_back = jax.vjp(norm_rows, inputs_f, gain_one)
    d_inputs_norm, grad_gain_one = norm_one_back(d_normed)
    input_grad = d_middle + d_inputs_norm
    summed = (
        lax.psum_scatter(grad_input, "dp", scatter_dimension=0, tiled=True),
        lax.psum_scatter(grad_gelu, "dp", scatter_dimension=0, tiled=True),
        lax.psum_scatter(grad_mixer, "dp", scatter_dimension=1, tiled=True),
        lax.psum_scatter(grad_gate, "dp", scatter_dimension=0, tiled=True),
        lax.psum_scatter(grad_upward, "dp", scatter_dimension=0, tiled=True),
        lax.psum_scatter(grad_down, "dp", scatter_dimension=1, tiled=True),
    )
    small = lax.psum(
        (
            grad_kernel,
            grad_bias,
            grad_alpha,
            grad_alpha_bias,
            grad_update,
            grad_update_bias,
            grad_decay,
        ),
        "dp",
    )
    gains = lax.psum((grad_gain_one, grad_gain_two), ("dp", "tensor"))
    return (
        block_output,
        input_grad,
        gains[0],
        summed[0],
        summed[1],
        small[0],
        small[1],
        small[2],
        small[3],
        small[4],
        small[5],
        small[6],
        summed[2],
        gains[1],
        summed[3],
        summed[4],
        summed[5],
    )


def solution(mesh):
    in_specs = (
        P(("dp", "tensor"), None),
        P("dp", None),
        P(("dp", "tensor"), None),
        P(),
        P("dp", "tensor"),
        P("dp", "tensor"),
        P(None, "tensor"),
        P("tensor"),
        P("tensor", None, None),
        P("tensor"),
        P("tensor", None, None),
        P("tensor"),
        P("tensor"),
        P("tensor", "dp"),
        P(),
        P("dp", "tensor"),
        P("dp", "tensor"),
        P("tensor", "dp"),
    )
    out_specs = (
        P(("dp", "tensor"), None),
        P(("dp", "tensor"), None),
        P(),
        P("dp", "tensor"),
        P("dp", "tensor"),
        P(None, "tensor"),
        P("tensor"),
        P("tensor", None, None),
        P("tensor"),
        P("tensor", None, None),
        P("tensor"),
        P("tensor"),
        P("tensor", "dp"),
        P(),
        P("dp", "tensor"),
        P("dp", "tensor"),
        P("tensor", "dp"),
    )
    return jax.shard_map(body, mesh=mesh, in_specs=in_specs, out_specs=out_specs, check_vma=False)
```

profile of v0, /device:TPU:0, one launch (start us, length us, event | category | flops | bytes accessed | tf_op | source)
XLA Modules:
  0.0 2555.8 jit_solution(4981652886541154451)
XLA Ops:
  14.7 30.6 %all-gather.11.cloned.1.call-done = bf16[2560,640]{1,0:T(8,128)(2,1)} async-done(((bf16[320,640]{1,0:T(8,128)(2,1)}), bf16[2560,640]{1,0:T(8,128)(2,1)}) %all-gather.11.cloned.1.call-update) | async-done | bytes 3276816 | tf_op jit(solution)/shard_map/all_gather | solution.py:95
  45.4 100.2 %all-gather.9.cloned.1.call-done = bf16[1024,2560]{1,0:T(8,128)(2,1)} async-done(((bf16[256,2560]{1,0:T(8,128)(2,1)}), bf16[1024,2560]{1,0:T(8,128)(2,1)}) %all-gather.9.cloned.1.call-update) | async-done | bytes 5242896 | tf_op jit(solution)/shard_map/all_gather | solution.py:119
  145.6 7.1 fusion.96
  161.7 4.8 fusion.97
  169.7 6.1 exponential_multiply_fusion
  175.8 7.1 slice.520
  183.0 7.1 slice.521
  198.3 4.3 fusion.77
  292.8 4.3 slice.524
  297.0 4.3 slice.589
  307.0 7.2 slice.591
  323.2 9.1 pad.169
  335.5 9.3 pad.168
  344.8 10.8 fusion.30
  355.6 10.7 fusion.99
  372.7 354.1 %all-reduce.61.cloned.1.call-done = f32[1024,2560]{1,0:T(8,128)} async-done(((f32[1024,2560]{1,0:T(8,128)}), f32[1024,2560]{1,0:T(8,128)}) %all-reduce.61.cloned.1.call-update) | async-done | bytes 10485776 | tf_op jit(solution)/shard_map/psum | solution.py:143
  726.8 4.9 multiply_reduce_fusion.1
  737.1 50.8 %all-gather.17.cloned.1.call-done = bf16[2560,1920]{1,0:T(8,128)(2,1)} async-done(((bf16[320,1920]{1,0:T(8,128)(2,1)}), bf16[2560,1920]{1,0:T(8,128)(2,1)}) %all-gather.17.cloned.1.call-update) | async-done | bytes 9830416 | tf_op jit(solution)/shard_map/all_gather | solution.py:98
  787.9 17.6 fusion.100
  805.5 44.7 %all-gather.19.cloned.1.call-done = bf16[2560,1920]{1,0:T(8,128)(2,1)} async-done(((bf16[320,1920]{1,0:T(8,128)(2,1)}), bf16[2560,1920]{1,0:T(8,128)(2,1)}) %all-gather.19.cloned.1.call-update) | async-done | bytes 9830416 | tf_op jit(solution)/shard_map/all_gather | solution.py:99
  850.1 17.1 fusion.101
  867.2 82.5 %all-gather.23.cloned.1.call-done = bf16[1024,2560]{1,0:T(8,128)(2,1)} async-done(((bf16[256,2560]{1,0:T(8,128)(2,1)}), bf16[1024,2560]{1,0:T(8,128)(2,1)}) %all-gather.23.cloned.1.call-update) | async-done | bytes 5242896 | tf_op jit(solution)/shard_map/all_gather | solution.py:154
  949.8 60.6 %all-gather.21.cloned.1.call-done = bf16[1920,2560]{0,1:T(8,128)(2,1)} async-done(((bf16[1920,320]{0,1:T(8,128)(2,1)}), bf16[1920,2560]{0,1:T(8,128)(2,1)}) %all-gather.21.cloned.1.call-update) | async-done | bytes 9830416 | tf_op jit(solution)/shard_map/all_gather | solution.py:100
  1010.4 26.8 %multiply_convert_fusion.1 = (bf16[1024,1920]{1,0:T(8,128)(2,1)}, bf16[1024,1920]{1,0:T(8,128)(2,1)}, bf16[1024,1920]{1,0:T(8,128)(2,1)}) fusion(f32[1024,1920]{1,0:T(8,128)} %fusion.100, f32[1024,1920]{1,0:T(8,128)} %fusion.101, bf16[1024,2560]{1,0:T(8,128)(2,1)} %all-gather.23.cloned.1.call-done, bf16[1920,2560]{0,1:T(8,128)(2,1)} %all-gather.21.cloned.1.call-done), kind=kOutput, calls=%fused_computation.14 | convolution fusion | flops 10117447680 | bytes 42598400 | tf_op jit(solution)/shard_map/dot_general | solution.py:69
  1037.2 17.4 fusion.103
  1054.7 17.0 convolution_add_fusion
  1071.7 17.1 fusion.102
  1091.9 4.6 slice.596
  1104.8 10.8 slice.597
  1115.6 10.9 slice.602
  1126.4 11.1 slice.595
  1141.0 289.3 %all-reduce.63.cloned.1.call-done = f32[1024,2560]{1,0:T(8,128)} async-done(((f32[1024,2560]{1,0:T(8,128)}), f32[1024,2560]{1,0:T(8,128)}) %all-reduce.63.cloned.1.call-update) | async-done | bytes 10485776 | tf_op jit(solution)/shard_map/psum | solution.py:163
  1430.3 8.1 multiply_reduce_fusion
  1438.4 10.7 fusion
  1449.6 7.5 fusion.20
  1457.1 17.1 reverse.6
  1482.5 4.3 fusion.76
  1578.7 4.3 slice.603
  1583.0 4.3 slice.668
  1608.2 9.2 pad.189
  1620.5 9.3 pad.188
  1633.3 21.0 rev.8
  1654.4 8.4 convert_reduce_fusion
  1675.8 7.8 fusion.73
  1687.6 4.3 fusion.104
  1691.9 7.0 convolution_add_fusion.1
  1705.2 10.0 fusion.105
  1716.6 11.0 fusion.34
  1728.9 9.6 fusion.106
  1738.8 18.0 fusion.109
  1756.8 17.9 fusion.110
  1775.0 18.0 fusion.111
  1795.1 25.9 %all-reduce.55 = (f32[4,640]{1,0:T(4,128)}, f32[640]{0:T(1024)}, f32[640]{0:T(1024)}, f32[640]{0:T(1024)}, f32[640]{0:T(1024)}) all-reduce(f32[4,640]{1,0:T(4,128)S(1)} %pad_add_fusion, f32[640]{0:T(1024)S(1)} %get-tuple-element.19, f32[640]{0:T(1024)S(1)} %get-tuple-element.41, ...), channel_id=1, replica_groups=mesh['dp'=8,'tensor'=4] {'dp'}, use_global_device_ids=true, to_apply=%region_16.17 | all-reduce | flops 5120 | bytes 40960 | tf_op jit(solution)/shard_map/psum | solution.py:212
  1821.1 5.3 multiply_reduce_fusion.2
  1826.4 50.3 %reduce-scatter.11.cloned.1.call-done = f32[256,2560]{1,0:T(8,128)} async-done(((f32[1024,2560]{1,0:T(8,128)}), f32[256,2560]{1,0:T(8,128)}) %reduce-scatter.11.cloned.1.call-update) | async-done | bytes 2621456 | tf_op jit(solution)/shard_map/reduce_scatter | solution.py:195
  1879.4 42.0 %all-reduce.54 = (f32[2560]{0:T(1024)}, f32[2560]{0:T(1024)}) all-reduce(f32[2560]{0:T(1024)S(1)} %get-tuple-element.17, f32[2560]{0:T(1024)S(1)} %get-tuple-element.47), channel_id=1, replica_groups=mesh['dp'=8,'tensor'=4] {'dp','tensor'}, use_global_device_ids=true, to_apply=%region_9.10 | all-reduce | flops 5120 | bytes 40960 | tf_op jit(solution)/shard_map/psum | solution.py:224
  1921.4 4.8 fusion.23
  1926.3 17.2 all-reduce.65.cloned.1.call-done
  1943.4 66.1 %reduce-scatter.13.cloned.1.call-done = f32[320,640]{1,0:T(8,128)} async-done(((f32[2560,640]{1,0:T(8,128)}), f32[320,640]{1,0:T(8,128)}) %reduce-scatter.13.cloned.1.call-update) | async-done | bytes 819216 | tf_op jit(solution)/shard_map/reduce_scatter | solution.py:205
  2009.6 66.9 %reduce-scatter.17.cloned.1.call-done = f32[640,320]{0,1:T(8,128)} async-done(((f32[640,2560]{0,1:T(8,128)}), f32[640,320]{0,1:T(8,128)}) %reduce-scatter.17.cloned.1.call-update) | async-done | bytes 819216 | tf_op jit(solution)/shard_map/reduce_scatter | solution.py:207
  2076.5 66.9 %reduce-scatter.15.cloned.1.call-done = f32[320,640]{1,0:T(8,128)} async-done(((f32[2560,640]{1,0:T(8,128)}), f32[320,640]{1,0:T(8,128)}) %reduce-scatter.15.cloned.1.call-update) | async-done | bytes 819216 | tf_op jit(solution)/shard_map/reduce_scatter | solution.py:206
  2143.4 134.1 %reduce-scatter.19.cloned.1.call-done = f32[320,1920]{1,0:T(8,128)} async-done(((f32[2560,1920]{1,0:T(8,128)}), f32[320,1920]{1,0:T(8,128)}) %reduce-scatter.19.cloned.1.call-update) | async-done | bytes 2457616 | tf_op jit(solution)/shard_map/reduce_scatter | solution.py:208
  2277.5 134.1 %reduce-scatter.21.cloned.1.call-done = f32[320,1920]{1,0:T(8,128)} async-done(((f32[2560,1920]{1,0:T(8,128)}), f32[320,1920]{1,0:T(8,128)}) %reduce-scatter.21.cloned.1.call-update) | async-done | bytes 2457616 | tf_op jit(solution)/shard_map/reduce_scatter | solution.py:209
  2411.6 134.3 %reduce-scatter.23.cloned.1.call-done = f32[1920,320]{0,1:T(8,128)} async-done(((f32[1920,2560]{0,1:T(8,128)}), f32[1920,320]{0,1:T(8,128)}) %reduce-scatter.23.cloned.1.call-update) | async-done | bytes 2457616 | tf_op jit(solution)/shard_map/reduce_scatter | solution.py:210
  (519 shorter events, 324.0 us)
Async XLA Ops:
  7.2 149.9 %copy-start = (bf16[2,320,320]{2,1,0:T(8,128)(2,1)S(1)}, bf16[2,320,320]{2,1,0:T(8,128)(2,1)}, u32[]{:S(2)}) copy-start(bf16[2,320,320]{2,1,0:T(8,128)(2,1)} %param.26) | copy-start | bytes 1228804
  7.2 38.2 %all-gather.11.cloned.1.call-start = ((), (), s32[]{:S(2)}) async-start(), calls=%async_computation.9 | async-start | bytes 3686400 | tf_op jit(solution)/shard_map/all_gather | solution.py:95
  8.0 137.7 %all-gather.9.cloned.1.call-start = ((), (), s32[]{:S(2)}) async-start(), calls=%async_computation.8 | async-start | bytes 6553600 | tf_op jit(solution)/shard_map/all_gather | solution.py:119
  13.0 331.8 %all-gather.13.cloned.1.call-start = ((), (), s32[]{:S(2)}) async-start(), calls=%async_computation.10 | async-start | bytes 3686400 | tf_op jit(solution)/shard_map/all_gather | solution.py:96
  13.7 341.9 %all-gather.15.cloned.1.call-start = ((), (), s32[]{:S(2)}) async-start(), calls=%async_computation.11 | async-start | bytes 3686400 | tf_op jit(solution)/shard_map/all_gather | solution.py:97
  14.3 712.5 %all-reduce.61.cloned.1.call-start = ((), (), s32[]{:S(2)}) async-start(), calls=%async_computation.12 | async-start | bytes 20971520 | tf_op jit(solution)/shard_map/psum | solution.py:143
  14.4 138.3 %copy-start.56 = (f32[640]{0:T(1024)}, f32[640]{0:T(1024)S(1)}, u32[]{:S(2)}) copy-start(f32[640]{0:T(1024)S(1)} %get-tuple-element.24) | copy-start | bytes 7684
  14.4 138.3 %copy-start.58 = (f32[640]{0:T(1024)}, f32[640]{0:T(1024)S(1)}, u32[]{:S(2)}) copy-start(f32[640]{0:T(1024)S(1)} %get-tuple-element.27) | copy-start | bytes 7684
  14.4 138.3 %copy-start.60 = (f32[640]{0:T(1024)}, f32[640]{0:T(1024)S(1)}, u32[]{:S(2)}) copy-start(f32[640]{0:T(1024)S(1)} %get-tuple-element.25) | copy-start | bytes 7684
  14.5 138.3 %copy-start.62 = (f32[640]{0:T(1024)}, f32[640]{0:T(1024)S(1)}, u32[]{:S(2)}) copy-start(f32[640]{0:T(1024)S(1)} %get-tuple-element.26) | copy-start | bytes 7684
  14.6 138.2 %copy-start.49 = (f32[1,1024]{1,0:T(1,128)}, f32[1,1024]{1,0:T(1,128)S(1)}, u32[]{:S(2)}) copy-start(f32[1,1024]{1,0:T(1,128)S(1)} %get-tuple-element.96) | copy-start | bytes 12292
  14.6 138.2 %copy-start.51 = (f32[1,1024]{1,0:T(1,128)}, f32[1,1024]{1,0:T(1,128)S(1)}, u32[]{:S(2)}) copy-start(f32[1,1024]{1,0:T(1,128)S(1)} %get-tuple-element.97) | copy-start | bytes 12292
  14.6 155.0 %copy-start.34 = (f32[1,1024]{1,0:T(1,128)}, f32[1,1024]{1,0:T(1,128)S(1)}, u32[]{:S(2)}) copy-start(f32[1,1024]{1,0:T(1,128)S(1)} %get-tuple-element.95) | copy-start | bytes 12292
  14.6 155.0 %copy-start.43 = (f32[1024]{0:T(1024)}, f32[1024]{0:T(1024)S(1)}, u32[]{:S(2)}) copy-start(f32[1024]{0:T(1024)S(1)} %broadcast_subtract_fusion) | copy-start | bytes 12292
  14.7 155.0 %copy-start.40 = (f32[640]{0:T(1024)}, f32[640]{0:T(1024)S(1)}, u32[]{:S(2)}) copy-start(f32[640]{0:T(1024)S(1)} %convert_element_type.91) | copy-start | bytes 7684
  14.7 154.9 %copy-start.45 = (f32[640]{0:T(1024)}, f32[640]{0:T(1024)S(1)}, u32[]{:S(2)}) copy-start(f32[640]{0:T(1024)S(1)} %broadcast_multiply_fusion) | copy-start | bytes 7684
  14.7 154.9 %copy-start.47 = (f32[640]{0:T(1024)}, f32[640]{0:T(1024)S(1)}, u32[]{:S(2)}) copy-start(f32[640]{0:T(1024)S(1)} %convert_element_type.90) | copy-start | bytes 7684
  175.8 14.2 copy-start.11
  306.8 9.5 copy-start.54
  306.9 9.5 copy-start.55
  306.9 9.5 copy-start.80
  306.9 9.6 copy-start.42
  306.9 9.6 copy-start.79
  306.9 9.7 copy-start.38
  306.9 9.7 copy-start.39
  306.9 9.7 copy-start.81
  306.9 9.8 copy-start.33
  306.9 9.8 copy-start.82
  306.9 9.9 copy-start.29
  307.0 9.9 copy-start.30
  307.0 9.9 copy-start.77
  335.5 9.4 copy-start.18
  355.6 10.7 copy-start.9
  369.8 418.0 %all-gather.17.cloned.1.call-start = ((), (), s32[]{:S(2)}) async-start(), calls=%async_computation.13 | async-start | bytes 11059200 | tf_op jit(solution)/shard_map/all_gather | solution.py:98
  370.4 479.7 %all-gather.19.cloned.1.call-start = ((), (), s32[]{:S(2)}) async-start(), calls=%async_computation.14 | async-start | bytes 11059200 | tf_op jit(solution)/shard_map/all_gather | solution.py:99
  371.2 578.6 %all-gather.23.cloned.1.call-start = ((), (), s32[]{:S(2)}) async-start(), calls=%async_computation.17 | async-start | bytes 6553600 | tf_op jit(solution)/shard_map/all_gather | solution.py:154
  371.9 638.5 %all-gather.21.cloned.1.call-start = ((), (), s32[]{:S(2)}) async-start(), calls=%async_computation.15 | async-start | bytes 11059200 | tf_op jit(solution)/shard_map/all_gather | solution.py:100
  372.7 1057.7 %all-reduce.63.cloned.1.call-start = ((), (), s32[]{:S(2)}) async-start(), calls=%async_computation.18 | async-start | bytes 20971520 | tf_op jit(solution)/shard_map/psum | solution.py:163
  1010.4 44.3 %slice-start = ((s8[9830400]{0:T(1024)(128)(4,1)}), s8[1441792]{0:T(1024)(128)(4,1)S(1)}, s32[]{:S(2)}) async-start(s8[9830400]{0:T(1024)(128)(4,1)} %bitcast.123), calls=%async_computation.27 | async-start | bytes 2883584
  1010.4 44.3 %slice-start.1 = ((s8[9830400]{0:T(1024)(128)(4,1)}), s8[4194304]{0:T(1024)(128)(4,1)S(1)}, s32[]{:S(2)}) async-start(s8[9830400]{0:T(1024)(128)(4,1)} %bitcast.123), calls=%async_computation.28 | async-start | bytes 8388608
  1037.2 17.4 slice-start.2
  1071.7 749.4 %reduce-scatter.9.cloned.1.call-start = ((), (), s32[]{:S(2)}) async-start(), calls=%async_computation.16 | async-start | bytes 13107200 | tf_op jit(solution)/shard_map/reduce_scatter | solution.py:150
  1088.9 787.8 %reduce-scatter.11.cloned.1.call-start = ((), (), s32[]{:S(2)}) async-start(), calls=%async_computation.19 | async-start | bytes 13107200 | tf_op jit(solution)/shard_map/reduce_scatter | solution.py:195
  1115.6 21.9 copy-start.19
  1438.4 10.8 copy-start.20
  1438.4 10.8 copy-start.96
  1438.4 11.2 copy-start.100
  1633.3 21.0 copy-start.5
  1633.3 21.0 copy-start.41
  1633.3 21.0 copy-start.44
  1633.3 21.0 copy-start.46
  1633.3 21.0 copy-start.48
  1699.0 244.5 %all-reduce.65.cloned.1.call-start = ((), (), s32[]{:S(2)}) async-start(), calls=%async_computation.26 | async-start | bytes 3932160 | tf_op jit(solution)/shard_map/psum | solution.py:212
  1705.1 304.4 %reduce-scatter.13.cloned.1.call-start = ((), (), s32[]{:S(2)}) async-start(), calls=%async_computation.20 | async-start | bytes 7372800 | tf_op jit(solution)/shard_map/reduce_scatter | solution.py:205
  1715.2 361.3 %reduce-scatter.17.cloned.1.call-start = ((), (), s32[]{:S(2)}) async-start(), calls=%async_computation.22 | async-start | bytes 7372800 | tf_op jit(solution)/shard_map/reduce_scatter | solution.py:207
  1727.6 415.8 %reduce-scatter.15.cloned.1.call-start = ((), (), s32[]{:S(2)}) async-start(), calls=%async_computation.21 | async-start | bytes 7372800 | tf_op jit(solution)/shard_map/reduce_scatter | solution.py:206
  1738.5 539.0 %reduce-scatter.19.cloned.1.call-start = ((), (), s32[]{:S(2)}) async-start(), calls=%async_computation.23 | async-start | bytes 22118400 | tf_op jit(solution)/shard_map/reduce_scatter | solution.py:208
  1756.8 654.9 %reduce-scatter.21.cloned.1.call-start = ((), (), s32[]{:S(2)}) async-start(), calls=%async_computation.24 | async-start | bytes 22118400 | tf_op jit(solution)/shard_map/reduce_scatter | solution.py:209
  1774.7 771.2 %reduce-scatter.23.cloned.1.call-start = ((), (), s32[]{:S(2)}) async-start(), calls=%async_computation.25 | async-start | bytes 22118400 | tf_op jit(solution)/shard_map/reduce_scatter | solution.py:210
  1821.1 55.7 %copy-start.10 = (bf16[256,2560]{1,0:T(8,128)(2,1)S(1)}, bf16[256,2560]{1,0:T(8,128)(2,1)}, u32[]{:S(2)}) copy-start(bf16[256,2560]{1,0:T(8,128)(2,1)} %param.18) | copy-start | bytes 3932164
  1821.1 55.7 %copy-start.37 = (f32[2560]{0:T(1024)S(1)}, f32[2560]{0:T(1024)}, u32[]{:S(2)}) copy-start(f32[2560]{0:T(1024)} %copy-done.36) | copy-start | bytes 30724
  1821.1 55.7 %copy-start.68 = (f32[256]{0:T(256)S(1)}, f32[256]{0:T(256)}, u32[]{:S(2)}) copy-start(f32[256]{0:T(256)} %copy-done.67) | copy-start | bytes 3076
  1826.4 95.0 %copy-start.86 = (f32[256]{0:T(256)S(1)}, f32[256]{0:T(256)}, u32[]{:S(2)}) copy-start(f32[256]{0:T(256)} %copy-done.85) | copy-start | bytes 3076
  1943.4 604.7 %copy-start.28 = (f32[2,320,320]{2,1,0:T(8,128)S(1)}, f32[2,320,320]{2,1,0:T(8,128)}, u32[]{:S(2)}) copy-start(f32[2,320,320]{2,1,0:T(8,128)} %get-tuple-element.111) | copy-start | bytes 2457604
  (59 other events, 218.7 us)
Sparse Core Ops, SparseCore 0:
  9.9 35.4 all-gather.10
  47.5 98.0 all-gather.8
  147.5 31.0 all-gather.12
  180.3 32.7 all-gather.14
  369.9 356.8 all-reduce.60
  728.5 59.2 all-gather.16
  789.8 60.3 all-gather.18
  851.7 98.0 all-gather.22
  951.7 58.6 all-gather.20
  1071.8 358.4 all-reduce.62
  1432.7 176.9 reduce-scatter.8
  1699.1 177.6 reduce-scatter.10
  1881.2 62.1 all-reduce.64
  1947.3 62.2 reduce-scatter.12
  2013.5 62.9 reduce-scatter.16
  2080.4 63.0 reduce-scatter.14
  2147.5 129.9 reduce-scatter.18
  2281.6 129.9 reduce-scatter.20
  2415.9 129.9 reduce-scatter.22
where the time goes:
time: 2580 us; the launch traced here: 2560 us
  waiting for transfers between devices  1690 us (66%)
  local copies, waits for them, and re-layouts  381 us (15%)
  matrix products  260 us (10%)
  other arithmetic  141 us (5%)
  blocking collectives  67.9 us (3%)
    psum x1, waiting for transfers between devices, body(): middle_all = lax.psum(placed, 'tensor')  354 us
    psum x1, waiting for transfers between devices, body(): d_second_all = lax.psum(second_terms, 'tensor')  289 us
    slice x63, local copies, waits for them, and re-layouts, body(): lax.associative_scan(linked, (decay_next, d_states), reverse=True, axis=1)  147 us
    reduce_scatter x1, waiting for transfers between devices, body(): lax.psum_scatter(grad_down, 'dp', scatter_dimension=1, tiled=True)  134 us
    reduce_scatter x1, waiting for transfers between devices, body(): lax.psum_scatter(grad_upward, 'dp', scatter_dimension=0, tiled=True)  134 us
    reduce_scatter x1, waiting for transfers between devices, body(): lax.psum_scatter(grad_gate, 'dp', scatter_dimension=0, tiled=True)  134 us
    slice x60, local copies, waits for them, and re-layouts, body(): states = lax.associative_scan(linked, (decay, driven), axis=1)[1]  122 us
    all_gather x1, waiting for transfers between devices, body(): normed_all = lax.all_gather(normed, 'tensor', axis=0, tiled=True)  100 us
  transfers between devices with their start and end apart: 19, of which 16 were waited for; matrix products, arithmetic and copies ran while one was open for 27% of the time, Pallas kernels for 0%

commit v1 on v0

v1 whole, which is shorter than its diff:
```python
from functools import partial

import jax
import jax.numpy as jnp
from jax import lax
from jax.experimental import pallas as pl
from jax.experimental.pallas import tpu as pltpu
from jax.sharding import PartitionSpec as P

EPSILON = 1e-06
RATE_SCALE = 8.0
GELU_C = 0.7978845608028654
GELU_A = 0.044715
GROUP = 8

F32 = jnp.float32
BF16 = jnp.bfloat16


def norm_rows(values, gain):
    inverse = lax.rsqrt(jnp.mean(values * values, axis=-1, keepdims=True) + EPSILON)
    return values * inverse * gain


def gated_hidden(gate_vals, up_vals):
    return jax.nn.gelu(gate_vals, approximate=True) * up_vals


def matmul(left, right):
    return jnp.dot(left, right, preferred_element_type=F32)


def inner_rows(left, right):
    return lax.dot_general(left, right, (((0,), (0,)), ((), ())), preferred_element_type=F32)


def times_transposed(left, right):
    return lax.dot_general(left, right, (((1,), (1,)), ((), ())), preferred_element_type=F32)


def mask_table(segment, taps):
    length = segment.shape[0]
    same, ahead = [], []
    for offset in range(1, taps):
        equal = (segment[offset:] == segment[:-offset]).astype(F32)
        same.append(jnp.pad(equal, (offset, 0)))
        ahead.append(jnp.pad(equal, (0, offset)))
    table = jnp.stack(same + ahead, axis=1)
    return jnp.pad(table, ((0, 0), (0, 8 - table.shape[1])))


def gelu_parts(v):
    th = jnp.tanh(GELU_C * (v + GELU_A * (v * v * v)))
    return 0.5 * (1.0 + th), th


def gate_terms(conv_f, pre, rate, keep, channels):
    alpha = jax.nn.sigmoid(pre[:, :channels])
    update = jax.nn.sigmoid(pre[:, channels:])
    log_decay = -rate * alpha
    th = jnp.tanh(log_decay)
    gap = (-2.0 * th) / (1.0 - th)
    return alpha, update, jnp.exp(log_decay), gap


def group_scan(a, b, reverse):
    rows, channels = a.shape
    a = a.reshape(rows // GROUP, GROUP, channels)
    b = b.reshape(rows // GROUP, GROUP, channels)
    place = lax.broadcasted_iota(jnp.int32, a.shape, 1)
    shift = 1
    while shift < GROUP:
        if reverse:
            inside = place < GROUP - shift
            step = GROUP - shift
        else:
            inside = place >= shift
            step = shift
        b_far = jnp.where(inside, pltpu.roll(b, step, 1), 0.0)
        a_far = jnp.where(inside, pltpu.roll(a, step, 1), 1.0)
        b = a * b_far + b
        a = a * a_far
        shift *= 2
    return a.reshape(rows, channels), b.reshape(rows, channels)


def forward_kernel(
    order, bg, table, taps, conv_bias, gate_w, gate_b, rate, mixed, states, conv_low, ext, carry, a_s, b_s
):
    step = pl.program_id(0)
    rows, channels = states.shape[1], states.shape[2]

    @pl.when(step == 0)
    def _():
        ext[0:8, :] = jnp.zeros((8, channels), F32)
        carry[...] = jnp.zeros((8, channels), F32)

    branch = bg[0, :, :channels]
    ext[8 : 8 + rows, :] = branch
    conv = branch * taps[0:1, :] + conv_bias[...]
    for k in range(1, 4):
        conv = conv + ext[8 - k : 8 - k + rows, :] * table[:, k - 1 : k] * taps[k : k + 1, :]
    ext[0:8, :] = ext[rows : rows + 8, :]
    low = conv.astype(BF16)
    conv_low[0] = low
    pre = matmul(low, gate_w[...]) + gate_b[...]
    keep = table[:, 0:1]
    conv_f = low.astype(F32)
    alpha, update, e, gap = gate_terms(conv_f, pre, rate[...], keep, channels)
    driven = conv_f * update * (keep * jnp.sqrt(gap) + (1.0 - keep))
    a, b = group_scan(keep * e, driven, False)
    a_s[...] = a
    b_s[...] = b

    def advance(g, held):
        at = pl.ds(pl.multiple_of(g * GROUP, GROUP), GROUP)
        now = a_s[at, :] * held + b_s[at, :]
        b_s[at, :] = now
        return jnp.broadcast_to(now[GROUP - 1 : GROUP, :], (GROUP, channels))

    carry[...] = lax.fori_loop(0, rows // GROUP, advance, carry[...], unroll=4)
    state = b_s[...]
    states[0] = state
    gate = bg[0, :, channels:]
    half, _ = gelu_parts(gate)
    mixed[0] = (state * (gate * half)).astype(BF16)


def recurrent_forward(order, bg, table, taps, conv_bias, gate_w, gate_b, rate):
    parts, rows, wide = bg.shape
    channels = wide // 2
    spun = lambda i, o: (o[i], 0, 0)
    whole = lambda i, o: (0, 0)
    return pl.pallas_call(
        forward_kernel,
        grid_spec=pltpu.PrefetchScalarGridSpec(
            num_scalar_prefetch=1,
            grid=(parts,),
            in_specs=[
                pl.BlockSpec((1, rows, wide), spun),
                pl.BlockSpec((rows, 8), lambda i, o: (i, 0)),
                pl.BlockSpec(taps.shape, whole),
                pl.BlockSpec(conv_bias.shape, whole),
                pl.BlockSpec(gate_w.shape, whole),
                pl.BlockSpec(gate_b.shape, whole),
                pl.BlockSpec(rate.shape, whole),
            ],
            out_specs=[
                pl.BlockSpec((1, rows, channels), spun),
                pl.BlockSpec((1, rows, channels), spun),
                pl.BlockSpec((1, rows, channels), spun),
            ],
            scratch_shapes=[
                pltpu.VMEM((rows + 8, channels), F32),
                pltpu.VMEM((8, channels), F32),
                pltpu.VMEM((rows, channels), F32),
                pltpu.VMEM((rows, channels), F32),
            ],
        ),
        out_shape=[
            jax.ShapeDtypeStruct((parts, rows, channels), BF16),
            jax.ShapeDtypeStruct((parts, rows, channels), F32),
            jax.ShapeDtypeStruct((parts, rows, channels), BF16),
        ],
        compiler_params=pltpu.CompilerParams(
            dimension_semantics=("arbitrary",), vmem_limit_bytes=48 << 20
        ),
        cost_estimate=pl.CostEstimate(
            flops=parts * rows * channels * (4 * channels + 200),
            bytes_accessed=parts * rows * channels * 16,
            transcendentals=parts * rows * channels * 6,
        ),
        name="recurrent_forward",
    )(order, bg, table, taps, conv_bias, gate_w, gate_b, rate)


def rows_to_groups(values):
    rows, channels = values.shape
    return jnp.sum(values.reshape(rows // GROUP, GROUP, channels), axis=0)


def backward_kernel(
    order, d_mixed, bg, before_bg, state_in, before_state, conv_low, table, taps, gate_w, gate_b, rate,
    d_bg, grad_w, sums, bias_sums, ext, shifted, carry, d_head, a_s, b_s,
):
    step = pl.program_id(0)
    rows, channels = state_in.shape[1], state_in.shape[2]

    @pl.when(step == 0)
    def _():
        carry[...] = jnp.zeros(carry.shape, F32)
        d_head[...] = jnp.zeros(d_head.shape, F32)
        grad_w[...] = jnp.zeros(grad_w.shape, F32)
        sums[...] = jnp.zeros(sums.shape, F32)
        bias_sums[...] = jnp.zeros(bias_sums.shape, F32)

    keep = table[:, 0:1]
    low = conv_low[0]
    conv_f = low.astype(F32)
    pre = matmul(low, gate_w[...]) + gate_b[...]
    alpha, update, e, gap = gate_terms(conv_f, pre, rate[...], keep, channels)
    root = jnp.sqrt(gap)
    scaling = keep * root + (1.0 - keep)
    decay = keep * e
    gate = bg[0, :, channels:]
    half, th = gelu_parts(gate)
    slope = half + 0.5 * gate * (1.0 - th * th) * (GELU_C * (1.0 + 3.0 * GELU_A * (gate * gate)))
    state = state_in[0]
    d_mix = d_mixed[0]
    d_state = d_mix * (gate * half)
    d_bg[0, :, channels:] = (d_mix * state * slope).astype(BF16)

    shifted[0:rows, :] = decay
    shifted[rows : rows + 8, :] = jnp.ones((8, channels), F32)
    a, b = group_scan(shifted[1 : 1 + rows, :], d_state, True)
    a_s[...] = a
    b_s[...] = b
    groups = rows // GROUP

    def advance(g, held):
        at = pl.ds(pl.multiple_of((groups - 1 - g) * GROUP, GROUP), GROUP)
        now = b_s[at, :] + a_s[at, :] * held
        b_s[at, :] = now
        return jnp.broadcast_to(now[0:1, :], (GROUP, channels))

    first = lax.fori_loop(0, groups, advance, carry[...], unroll=4)
    carry[...] = jnp.broadcast_to(decay[0:1, :], (GROUP, channels)) * first
    adjoint = b_s[...]

    ext[0:8, :] = before_state[0]
    ext[8 : 8 + rows, :] = state
    d_decay = adjoint * ext[7 : 7 + rows, :]
    d_direct = adjoint * update * scaling
    d_update = adjoint * conv_f * scaling * (update * (1.0 - update))
    d_log = keep * (e * d_decay - adjoint * conv_f * update * (e * e / root))
    by_rate = alpha * d_log
    d_alpha = -rate[...] * (by_rate * (1.0 - alpha))
    d_pre = jnp.concatenate([d_alpha, d_update], axis=1).astype(BF16)
    grad_w[...] += inner_rows(low, d_pre)
    bias_sums[...] += rows_to_groups(d_pre.astype(F32))
    d_conv = d_direct + times_transposed(d_pre, gate_w[...])

    ext[0:8, :] = before_bg[0, :, :channels]
    ext[8 : 8 + rows, :] = bg[0, :, :channels]
    shifted[0:rows, :] = d_conv
    shifted[rows : rows + 8, :] = d_head[...]
    d_head[...] = d_conv[0:8, :]
    d_branch = d_conv * taps[0:1, :]
    sums[0] += rows_to_groups(d_conv * ext[8 : 8 + rows, :])
    for k in range(1, 4):
        sums[k] += rows_to_groups(d_conv * (ext[8 - k : 8 - k + rows, :] * table[:, k - 1 : k]))
        d_branch = d_branch + shifted[k : k + rows, :] * table[:, 2 + k : 3 + k] * taps[k : k + 1, :]
    sums[4] += rows_to_groups(d_conv)
    sums[5] += rows_to_groups(by_rate)
    d_bg[0, :, :channels] = d_branch.astype(BF16)


def recurrent_backward(order, d_mixed, bg, states, conv_low, table, taps, gate_w, gate_b, rate):
    parts, rows, wide = bg.shape
    channels = wide // 2
    last = rows // 8 - 1
    spun = lambda i, o: (o[parts - 1 - i], 0, 0)
    before = lambda i, o: (o[jnp.maximum(parts - 2 - i, 0)], last, 0)
    whole = lambda i, o: (0, 0)
    whole3 = lambda i, o: (0, 0, 0)
    return pl.pallas_call(
        backward_kernel,
        grid_spec=pltpu.PrefetchScalarGridSpec(
            num_scalar_prefetch=1,
            grid=(parts,),
            in_specs=[
                pl.BlockSpec((1, rows, channels), spun),
                pl.BlockSpec((1, rows, wide), spun),
                pl.BlockSpec((1, 8, wide), before),
                pl.BlockSpec((1, rows, channels), spun),
                pl.BlockSpec((1, 8, channels), before),
                pl.BlockSpec((1, rows, channels), spun),
                pl.BlockSpec((rows, 8), lambda i, o: (parts - 1 - i, 0)),
                pl.BlockSpec(taps.shape, whole),
                pl.BlockSpec(gate_w.shape, whole),
                pl.BlockSpec(gate_b.shape, whole),
                pl.BlockSpec(rate.shape, whole),
            ],
            out_specs=[
                pl.BlockSpec((1, rows, wide), spun),
                pl.BlockSpec((channels, wide), whole),
                pl.BlockSpec((6, 8, channels), whole3),
                pl.BlockSpec((8, wide), whole),
            ],
            scratch_shapes=[
                pltpu.VMEM((rows + 8, channels), F32),
                pltpu.VMEM((rows + 8, channels), F32),
                pltpu.VMEM((8, channels), F32),
                pltpu.VMEM((8, channels), F32),
                pltpu.VMEM((rows, channels), F32),
                pltpu.VMEM((rows, channels), F32),
            ],
        ),
        out_shape=[
            jax.ShapeDtypeStruct((parts, rows, wide), BF16),
            jax.ShapeDtypeStruct((channels, wide), F32),
            jax.ShapeDtypeStruct((6, 8, channels), F32),
            jax.ShapeDtypeStruct((8, wide), F32),
        ],
        compiler_params=pltpu.CompilerParams(
            dimension_semantics=("arbitrary",), vmem_limit_bytes=48 << 20
        ),
        cost_estimate=pl.CostEstimate(
            flops=parts * rows * channels * (12 * channels + 300),
            bytes_accessed=parts * rows * channels * 24,
            transcendentals=parts * rows * channels * 6,
        ),
        name="recurrent_backward",
    )(order, d_mixed, bg, bg, states, states, conv_low, table, taps, gate_w, gate_b, rate)


def block_diagonal(weight):
    blocks, width, _ = weight.shape
    rows = [
        jnp.pad(weight[b], ((0, 0), (b * width, (blocks - 1 - b) * width))) for b in range(blocks)
    ]
    return jnp.concatenate(rows, axis=0)


def body(
    parts,
    block_input,
    segment_ids,
    output_cotangent,
    first_gain,
    input_weight,
    gelu_weight,
    conv_kernel,
    conv_bias,
    alpha_weight,
    alpha_bias,
    update_weight,
    update_bias,
    decay_param,
    mixer_weight,
    second_gain,
    gate_weight,
    up_weight,
    down_weight,
):
    rows = block_input.shape[0]
    channels = input_weight.shape[1]
    units = gate_weight.shape[1]
    blocks, block_width = alpha_weight.shape[0], alpha_weight.shape[1]
    ring = [(i, (i + 1) % parts) for i in range(parts)]

    def onward(values):
        return lax.ppermute(values, "tensor", ring)

    def gather_ring(own):
        held = [own]
        for _ in range(parts - 1):
            held.append(onward(held[-1]))
        return held

    def scatter_ring(terms):
        total = terms[1 % parts]
        for k in range(2, parts + 1):
            arrived = onward(total.astype(BF16))
            total = arrived.astype(F32) + terms[k % parts]
        return total

    me = lax.axis_index("tensor")
    order = lax.rem(me - jnp.arange(parts, dtype=jnp.int32) + parts, parts)

    w_in = lax.all_gather(jnp.concatenate([input_weight, gelu_weight], axis=1), "dp", axis=0, tiled=True)
    w_mix = lax.all_gather(mixer_weight.T, "dp", axis=0, tiled=True)
    w_ff = lax.all_gather(jnp.concatenate([gate_weight, up_weight], axis=1), "dp", axis=0, tiled=True)
    w_down = lax.all_gather(down_weight.T, "dp", axis=0, tiled=True)

    gain_one = first_gain.astype(F32)
    gain_two = second_gain.astype(F32)
    taps = conv_kernel.astype(F32)
    bias_f = conv_bias.astype(F32)[None, :]
    decay_f = decay_param.astype(F32)
    rate = (RATE_SCALE * jax.nn.softplus(decay_f))[None, :]
    gate_w = jnp.concatenate([block_diagonal(alpha_weight), block_diagonal(update_weight)], axis=1)
    gate_b = jnp.concatenate([alpha_bias, update_bias]).astype(F32)[None, :]
    table = mask_table(segment_ids[0], conv_kernel.shape[0])

    inputs_f = block_input.astype(F32)
    normed = norm_rows(inputs_f, gain_one).astype(BF16)
    normed_blocks = gather_ring(normed)
    bg = jnp.stack([matmul(block, w_in) for block in normed_blocks])
    mixed, states, conv_low = recurrent_forward(order, bg, table, taps, bias_f, gate_w, gate_b, rate)
    mix_terms = [lax.optimization_barrier(times_transposed(mixed[k], w_mix)) for k in range(parts)]
    middle = inputs_f + scatter_ring(mix_terms)
    second = norm_rows(middle, gain_two).astype(BF16)

    cot_blocks = gather_ring(output_cotangent)
    second_blocks = gather_ring(second)
    hidden_blocks, d_ff_blocks = [], []
    for k in range(parts):
        gate_up = matmul(second_blocks[k], w_ff)
        d_hidden = matmul(cot_blocks[k], w_down)
        hidden, hidden_back = jax.vjp(gated_hidden, gate_up[:, :units], gate_up[:, units:])
        d_gate, d_up = hidden_back(d_hidden)
        hidden_blocks.append(hidden.astype(BF16))
        d_ff_blocks.append(jnp.concatenate([d_gate, d_up], axis=1).astype(BF16))
    second_terms = [lax.optimization_barrier(times_transposed(d, w_ff)) for d in d_ff_blocks]
    d_second = scatter_ring(second_terms)
    out_terms = [lax.optimization_barrier(times_transposed(h, w_down)) for h in hidden_blocks]
    block_output = (middle + scatter_ring(out_terms)).astype(BF16)

    cot_all = jnp.concatenate(cot_blocks, axis=0)
    grad_down_t = inner_rows(cot_all, jnp.concatenate(hidden_blocks, axis=0)).astype(BF16)
    grad_ff = inner_rows(
        jnp.concatenate(second_blocks, axis=0), jnp.concatenate(d_ff_blocks, axis=0)
    ).astype(BF16)

    _, norm_two_back = jax.vjp(norm_rows, middle, gain_two)
    d_middle_norm, grad_gain_two = norm_two_back(d_second)
    d_middle = output_cotangent.astype(F32) + d_middle_norm
    d_middle_blocks = gather_ring(d_middle.astype(BF16))
    d_mixed = jnp.stack([matmul(d, w_mix) for d in d_middle_blocks])
    d_bg, grad_gates, sums, bias_sums = recurrent_backward(
        order, d_mixed, bg, states, conv_low, table, taps, gate_w, gate_b, rate
    )
    grad_mix_t = inner_rows(
        jnp.concatenate(d_middle_blocks, axis=0), mixed.reshape(parts * rows, channels)
    ).astype(BF16)
    grad_in = inner_rows(
        jnp.concatenate(normed_blocks, axis=0), d_bg.reshape(parts * rows, 2 * channels)
    ).astype(BF16)
    first_terms = [lax.optimization_barrier(times_transposed(d_bg[k], w_in)) for k in range(parts)]
    d_normed = scatter_ring(first_terms)
    _, norm_one_back = jax.vjp(norm_rows, inputs_f, gain_one)
    d_inputs_norm, grad_gain_one = norm_one_back(d_normed)
    input_grad = d_middle + d_inputs_norm

    def spread(grad):
        return lax.psum_scatter(grad, "dp", scatter_dimension=0, tiled=True).astype(F32)

    own_down = spread(grad_down_t).T
    own_ff = spread(grad_ff)
    own_mix = spread(grad_mix_t).T
    own_in = spread(grad_in)

    sums = jnp.sum(sums, axis=1)
    bias_sums = jnp.sum(bias_sums, axis=0)
    grad_kernel, grad_bias = sums[:4], sums[4]
    grad_decay = -RATE_SCALE * sums[5] * jax.nn.sigmoid(decay_f)

    def diagonal(start):
        return jnp.stack(
            [
                lax.slice(
                    grad_gates,
                    (b * block_width, start + b * block_width),
                    ((b + 1) * block_width, start + (b + 1) * block_width),
                )
                for b in range(blocks)
            ]
        )

    small = lax.psum(
        (
            grad_kernel,
            grad_bias,
            diagonal(0),
            bias_sums[:channels],
            diagonal(channels),
            bias_sums[channels:],
            grad_decay,
        ),
        "dp",
    )
    gains = lax.psum((grad_gain_one, grad_gain_two), ("dp", "tensor"))
    return (
        block_output,
        input_grad,
        gains[0],
        own_in[:, :channels],
        own_in[:, channels:],
        small[0],
        small[1],
        small[2],
        small[3],
        small[4],
        small[5],
        small[6],
        own_mix,
        gains[1],
        own_ff[:, :units],
        own_ff[:, units:],
        own_down,
    )


def solution(mesh):
    in_specs = (
        P(("dp", "tensor"), None),
        P("dp", None),
        P(("dp", "tensor"), None),
        P(),
        P("dp", "tensor"),
        P("dp", "tensor"),
        P(None, "tensor"),
        P("tensor"),
        P("tensor", None, None),
        P("tensor"),
        P("tensor", None, None),
        P("tensor"),
        P("tensor"),
        P("tensor", "dp"),
        P(),
        P("dp", "tensor"),
        P("dp", "tensor"),
        P("tensor", "dp"),
    )
    out_specs = (
        P(("dp", "tensor"), None),
        P(("dp", "tensor"), None),
        P(),
        P("dp", "tensor"),
        P("dp", "tensor"),
        P(None, "tensor"),
        P("tensor"),
        P("tensor", None, None),
        P("tensor"),
        P("tensor", None, None),
        P("tensor"),
        P("tensor"),
        P("tensor", "dp"),
        P(),
        P("dp", "tensor"),
        P("dp", "tensor"),
        P("tensor", "dp"),
    )
    return jax.shard_map(
        partial(body, mesh.shape["tensor"]),
        mesh=mesh,
        in_specs=in_specs,
        out_specs=out_specs,
        check_vma=False,
    )
```

time: 2580 us -> 1120 us (0.43)
  waiting for transfers between devices: 1690 us -> 675 us
  local copies, waits for them, and re-layouts: 381 us -> 24.9 us
  other arithmetic: 141 us -> 41.2 us
  Pallas kernels: 0 us -> 32.5 us
    psum x3 -> x1, waiting for transfers between devices: 661 us -> 61.2 us  [body(): lax.psum((grad_kernel, grad_bias, diagonal(0), bias_sums[:channels], diag...]
    reduce_scatter x8 -> x4, waiting for transfers between devices: 653 us -> 82.5 us  [spread(): lax.psum_scatter(grad, 'dp', scatter_dimension=0, tiled=True).astype(F32)]
    ppermute x0 -> x24, waiting for transfers between devices: none -> 530 us  [onward(): return lax.ppermute(values, 'tensor', ring)]
    all_gather x8 -> x4, waiting for transfers between devices: 369 us -> 0.03 us  [the longest x1 0.02 us: body(): lax.all_gather(jnp.concatenate([input_weight, gelu_weight], axis=1), 'dp'...]
    slice x125 -> x4, local copies, waits for them, and re-layouts: 270 us -> 6.81 us  [the longest x1 4.26 us: body(): own_ff[:, units:]]
    pad x36 -> x3, local copies, waits for them, and re-layouts: 42.6 us -> 0.2 us  [the longest x2 0.16 us: mask_table(): ahead.append(jnp.pad(equal, (0, offset)))]
    mul x23 -> x3, other arithmetic: 41.7 us -> 0.05 us  [the longest x2 0.03 us: body(): grad_decay = -RATE_SCALE * sums[5] * jax.nn.sigmoid(decay_f)]
    add x39 -> x0, other arithmetic: 32.6 us -> none  [the longest x1 10.7 us: body(): cotangent_all.astype(jnp.float32) + full_back(d_second_all)[0]]
  transfers between devices with their start and end apart: 19 -> 33, of which waited for: 16 -> 23; matrix products, arithmetic and copies ran while one was open for 27% -> 21% of each run, Pallas kernels for 0% -> 3%
where the time goes in v1:
time: 1120 us
  waiting for transfers between devices  675 us (60%)
  matrix products  252 us (22%)
  blocking collectives  63.8 us (6%)
  other arithmetic  41.2 us (4%)
  Pallas kernels  32.5 us (3%)
  local copies, waits for them, and re-layouts  24.9 us (2%)
  between operations  15.2 us (1%)
  starting transfers between devices  14.8 us (1%)
    ppermute x24, waiting for transfers between devices, onward(): return lax.ppermute(values, 'tensor', ring)  530 us
    dot_general x16, matrix products, matmul(): return jnp.dot(left, right, preferred_element_type=F32)  97.2 us
    dot_general x16, matrix products, times_transposed(): lax.dot_general(left, right, (((1,), (1,)), ((), ())), preferred_element_...  90.6 us
    reduce_scatter x4, waiting for transfers between devices, spread(): lax.psum_scatter(grad, 'dp', scatter_dimension=0, tiled=True).astype(F32)  82.5 us
    dot_general x4, matrix products, inner_rows(): lax.dot_general(left, right, (((0,), (0,)), ((), ())), preferred_element_...  64.2 us
    psum x1, waiting for transfers between devices, body(): lax.psum((grad_kernel, grad_bias, diagonal(0), bias_sums[:channels], diag...  61.2 us
    psum x1, blocking collectives, body(): gains = lax.psum((grad_gain_one, grad_gain_two), ('dp', 'tensor'))  39.2 us
    psum x1, blocking collectives, body(): lax.psum((grad_kernel, grad_bias, diagonal(0), bias_sums[:channels], diag...  24.6 us
  transfers between devices with their start and end apart: 33, of which 23 were waited for; matrix products, arithmetic and copies ran while one was open for 21% of the time, Pallas kernels for 3%

profile of v1, /device:TPU:0, one launch (start us, length us, event | category | flops | bytes accessed | tf_op | source)
XLA Modules:
  0.0 1119.5 jit_solution(15356434823808407742)
XLA Ops:
  10.3 3.0 pad_maximum_fusion.2
  14.8 3.1 collective-permute-start
  18.4 30.3 %collective-permute-done = bf16[256,2560]{1,0:T(8,128)(2,1)} collective-permute-done((bf16[256,2560]{1,0:T(8,128)(2,1)S(1)}, bf16[256,2560]{1,0:T(8,128)(2,1)}, u32[]{:S(2)}, u32[]{:S(2)}) %collective-permute-start) | collective-permute-done | bytes 1310752 | tf_op jit(solution)/shard_map/ppermute | solution.py:353
  50.6 4.0 fusion.119.gate_w
  54.6 26.2 %collective-permute-done.1 = bf16[256,2560]{1,0:T(8,128)(2,1)} collective-permute-done((bf16[256,2560]{1,0:T(8,128)(2,1)}, bf16[256,2560]{1,0:T(8,128)(2,1)}, u32[]{:S(2)}, u32[]{:S(2)}) %collective-permute-start.1) | collective-permute-done | bytes 1310752 | tf_op jit(solution)/shard_map/ppermute | solution.py:353
  81.2 5.7 convolution_bitcast_fusion.3
  86.9 3.2 convolution_bitcast_fusion.2
  90.1 3.2 convolution_bitcast_fusion.1
  93.3 19.0 %collective-permute-done.2 = bf16[256,2560]{1,0:T(8,128)(2,1)} collective-permute-done((bf16[256,2560]{1,0:T(8,128)(2,1)}, bf16[256,2560]{1,0:T(8,128)(2,1)}, u32[]{:S(2)}, u32[]{:S(2)}) %collective-permute-start.2) | collective-permute-done | bytes 1310752 | tf_op jit(solution)/shard_map/ppermute | solution.py:353
  112.3 3.2 convolution_bitcast_fusion
  118.2 11.3 %recurrent_forward.1 = (bf16[4,256,640]{2,1,0:T(8,128)(2,1)S(1)}, f32[4,256,640]{2,1,0:T(8,128)}, bf16[4,256,640]{2,1,0:T(8,128)(2,1)S(1)}) custom-call(s32[4]{0:T(128)S(1)} %compare_select_fusion.1.order, f32[4,256,1280]{2,1,0:T(8,128)} %pad_maximum_fusion.bg.before_bg, f32[1024,8]{1,0:T(8,128)S(1)} %pad.48.table, f32[4,640]{1,0:T(4,128)S(1)} %convert_element_type.196.taps, ...), custom_call_target="tpu_custom_call" | custom-call | flops 1808793600 | bytes 10485760 | tf_op jit(solution)/shard_map/recurrent_forward/pallas_call | solution.py:134
  130.6 3.4 fusion.139
  135.3 28.8 %collective-permute-done.3 = bf16[256,2560]{1,0:T(8,128)(2,1)S(1)} collective-permute-done((bf16[256,2560]{1,0:T(8,128)(2,1)S(1)}, bf16[256,2560]{1,0:T(8,128)(2,1)S(1)}, u32[]{:S(2)}, u32[]{:S(2)}) %collective-permute-start.3) | collective-permute-done | bytes 1310752 | tf_op jit(solution)/shard_map/ppermute | solution.py:353
  165.7 27.9 %collective-permute-done.4 = bf16[256,2560]{1,0:T(8,128)(2,1)S(1)} collective-permute-done((bf16[256,2560]{1,0:T(8,128)(2,1)S(1)}, bf16[256,2560]{1,0:T(8,128)(2,1)S(1)}, u32[]{:S(2)}, u32[]{:S(2)}) %collective-permute-start.4) | collective-permute-done | bytes 1310752 | tf_op jit(solution)/shard_map/ppermute | solution.py:353
  195.8 27.0 %collective-permute-done.5 = bf16[256,2560]{1,0:T(8,128)(2,1)S(1)} collective-permute-done((bf16[256,2560]{1,0:T(8,128)(2,1)S(1)}, bf16[256,2560]{1,0:T(8,128)(2,1)S(1)}, u32[]{:S(2)}, u32[]{:S(2)}) %collective-permute-start.5) | collective-permute-done | bytes 1310752 | tf_op jit(solution)/shard_map/ppermute | solution.py:353
  225.8 33.0 %collective-permute-done.6 = bf16[256,2560]{1,0:T(8,128)(2,1)S(1)} collective-permute-done((bf16[256,2560]{1,0:T(8,128)(2,1)S(1)}, bf16[256,2560]{1,0:T(8,128)(2,1)S(1)}, u32[]{:S(2)}, u32[]{:S(2)}) %collective-permute-start.6) | collective-permute-done | bytes 1310752 | tf_op jit(solution)/shard_map/ppermute | solution.py:353
  258.9 28.1 %collective-permute-done.12 = bf16[256,2560]{1,0:T(8,128)(2,1)S(1)} collective-permute-done((bf16[256,2560]{1,0:T(8,128)(2,1)S(1)}, bf16[256,2560]{1,0:T(8,128)(2,1)S(1)}, u32[]{:S(2)}, u32[]{:S(2)}) %collective-permute-start.12) | collective-permute-done | bytes 1310752 | tf_op jit(solution)/shard_map/ppermute | solution.py:353
  287.0 28.1 %collective-permute-done.8 = bf16[256,2560]{1,0:T(8,128)(2,1)S(1)} collective-permute-done((bf16[256,2560]{1,0:T(8,128)(2,1)S(1)}, bf16[256,2560]{1,0:T(8,128)(2,1)S(1)}, u32[]{:S(2)}, u32[]{:S(2)}) %collective-permute-start.8) | collective-permute-done | bytes 1310752 | tf_op jit(solution)/shard_map/ppermute | solution.py:353
  315.1 28.2 %collective-permute-done.14 = bf16[256,2560]{1,0:T(8,128)(2,1)} collective-permute-done((bf16[256,2560]{1,0:T(8,128)(2,1)S(1)}, bf16[256,2560]{1,0:T(8,128)(2,1)}, u32[]{:S(2)}, u32[]{:S(2)}) %collective-permute-start.14) | collective-permute-done | bytes 1310752 | tf_op jit(solution)/shard_map/ppermute | solution.py:353
  343.3 28.1 %collective-permute-done.10 = bf16[256,2560]{1,0:T(8,128)(2,1)} collective-permute-done((bf16[256,2560]{1,0:T(8,128)(2,1)S(1)}, bf16[256,2560]{1,0:T(8,128)(2,1)}, u32[]{:S(2)}, u32[]{:S(2)}) %collective-permute-start.10) | collective-permute-done | bytes 1310752 | tf_op jit(solution)/shard_map/ppermute | solution.py:353
  371.3 13.5 %fusion.178 = f32[256,3840]{1,0:T(8,128)} fusion(bf16[256,2560]{1,0:T(8,128)(2,1)} %collective-permute-done.10, bf16[2560,3840]{1,0:T(8,128)(2,1)} %all-gather.9.cloned.1.call-done), kind=kOutput, calls=%fused_computation.264 | convolution fusion | flops 5033164800 | bytes 24903680 | tf_op jit(solution)/shard_map/dot_general | solution.py:30
  384.9 8.6 collective-permute-done.16
  393.5 10.2 fusion.94
  404.6 9.8 fusion.110
  414.4 10.0 fusion.174
  424.4 9.2 fusion.80
  433.7 11.1 fusion.102
  444.7 7.9 fusion.175
  452.6 9.9 fusion.176
  462.6 9.7 fusion.180
  472.4 6.7 fusion.87
  479.1 5.3 fusion.101
  484.4 11.1 fusion.106
  495.5 10.3 fusion.114
  505.8 6.0 fusion.177
  515.9 4.3 collective-permute-start.9
  520.2 5.5 fusion.179
  525.8 21.2 %collective-permute-done.15 = bf16[256,2560]{1,0:T(8,128)(2,1)S(1)} collective-permute-done((bf16[256,2560]{1,0:T(8,128)(2,1)S(1)}, bf16[256,2560]{1,0:T(8,128)(2,1)S(1)}, u32[]{:S(2)}, u32[]{:S(2)}) %collective-permute-start.15) | collective-permute-done | bytes 1310752 | tf_op jit(solution)/shard_map/ppermute | solution.py:353
  548.0 27.1 %collective-permute-done.9 = bf16[256,2560]{1,0:T(8,128)(2,1)S(1)} collective-permute-done((bf16[256,2560]{1,0:T(8,128)(2,1)S(1)}, bf16[256,2560]{1,0:T(8,128)(2,1)S(1)}, u32[]{:S(2)}, u32[]{:S(2)}) %collective-permute-start.9) | collective-permute-done | bytes 1310752 | tf_op jit(solution)/shard_map/ppermute | solution.py:353
  576.1 5.7 fusion.181
  581.8 21.3 %collective-permute-done.17 = bf16[256,2560]{1,0:T(8,128)(2,1)S(1)} collective-permute-done((bf16[256,2560]{1,0:T(8,128)(2,1)S(1)}, bf16[256,2560]{1,0:T(8,128)(2,1)S(1)}, u32[]{:S(2)}, u32[]{:S(2)}) %collective-permute-start.17) | collective-permute-done | bytes 1310752 | tf_op jit(solution)/shard_map/ppermute | solution.py:353
  604.2 20.2 %collective-permute-done.11 = bf16[256,2560]{1,0:T(8,128)(2,1)S(1)} collective-permute-done((bf16[256,2560]{1,0:T(8,128)(2,1)S(1)}, bf16[256,2560]{1,0:T(8,128)(2,1)S(1)}, u32[]{:S(2)}, u32[]{:S(2)}) %collective-permute-start.11) | collective-permute-done | bytes 1310752 | tf_op jit(solution)/shard_map/ppermute | solution.py:353
  624.4 3.6 fusion.166
  629.2 27.7 %collective-permute-done.18 = bf16[256,2560]{1,0:T(8,128)(2,1)S(1)} collective-permute-done((bf16[256,2560]{1,0:T(8,128)(2,1)S(1)}, bf16[256,2560]{1,0:T(8,128)(2,1)S(1)}, u32[]{:S(2)}, u32[]{:S(2)}) %collective-permute-start.18) | collective-permute-done | bytes 1310752 | tf_op jit(solution)/shard_map/ppermute | solution.py:353
  658.1 27.8 %collective-permute-done.19 = bf16[256,2560]{1,0:T(8,128)(2,1)S(1)} collective-permute-done((bf16[256,2560]{1,0:T(8,128)(2,1)S(1)}, bf16[256,2560]{1,0:T(8,128)(2,1)S(1)}, u32[]{:S(2)}, u32[]{:S(2)}) %collective-permute-start.19) | collective-permute-done | bytes 1310752 | tf_op jit(solution)/shard_map/ppermute | solution.py:353
  687.1 22.8 %collective-permute-done.20 = bf16[256,2560]{1,0:T(8,128)(2,1)S(1)} collective-permute-done((bf16[256,2560]{1,0:T(8,128)(2,1)S(1)}, bf16[256,2560]{1,0:T(8,128)(2,1)S(1)}, u32[]{:S(2)}, u32[]{:S(2)}) %collective-permute-start.20) | collective-permute-done | bytes 1310752 | tf_op jit(solution)/shard_map/ppermute | solution.py:353
  711.0 6.0 fusion.44
  717.0 16.5 %convolution_convert_fusion.1 = bf16[2560,1920]{1,0:T(8,128)(2,1)} fusion(bf16[256,2560]{1,0:T(8,128)(2,1)} %collective-permute-done.16, bf16[256,2560]{1,0:T(8,128)(2,1)} %collective-permute-done.14, bf16[256,2560]{1,0:T(8,128)(2,1)} %copy-done.58, bf16[256,2560]{1,0:T(8,128)(2,1)} %param.20, bf16[256,1920]{1,0:T(8,128)(2,1)} %copy-done.66, ...), kind=kOutput, calls=%fused_computation.1 | convolution fusion | flops 10107944960 | bytes 19005440 | tf_op jit(solution)/shard_map/dot_general | solution.py:34
  733.6 3.7 convolution_bitcast_fusion.7
  743.4 21.2 %recurrent_backward.1 = (bf16[4,256,1280]{2,1,0:T(8,128)(2,1)}, f32[640,1280]{1,0:T(8,128)}, f32[6,8,640]{2,1,0:T(8,128)S(1)}, f32[8,1280]{1,0:T(8,128)S(1)}) custom-call(s32[4]{0:T(128)S(1)} %copy-done.10, f32[4,256,640]{2,1,0:T(8,128)} %pad_maximum_fusion.1.d_mixed, f32[4,256,1280]{2,1,0:T(8,128)} %pad_maximum_fusion.bg.before_bg, ...), custom_call_target="tpu_custom_call" | custom-call | flops 5229772800 | bytes 15728640 | tf_op jit(solution)/shard_map/recurrent_backward/pallas_call | solution.py:266
  765.3 11.5 %convolution_convert_fusion.2 = bf16[2560,1280]{1,0:T(8,128)(2,1)} fusion(bf16[1024,1280]{1,0:T(8,128)(2,1)} %bitcast.143, bf16[256,2560]{1,0:T(8,128)(2,1)} %collective-permute-done.2, bf16[256,2560]{1,0:T(8,128)(2,1)} %collective-permute-done.1, bf16[256,2560]{1,0:T(8,128)(2,1)} %collective-permute-done, bf16[256,2560]{1,0:T(8,128)(2,1)S(1)} %copy-done.27), kind=kOutput, calls=%fused_computation.2 | convolution fusion | flops 6735134720 | bytes 14417920 | tf_op jit(solution)/shard_map/dot_general | solution.py:34
  779.1 30.2 %convolution_convert_fusion = bf16[2560,3840]{1,0:T(8,128)(2,1)} fusion(bf16[256,1920]{1,0:T(8,128)(2,1)} %get-tuple-element.55, bf16[256,1920]{1,0:T(8,128)(2,1)} %copy-done.69, bf16[256,1920]{1,0:T(8,128)(2,1)} %get-tuple-element.53, bf16[256,1920]{1,0:T(8,128)(2,1)} %copy-done.70, bf16[256,1920]{1,0:T(8,128)(2,1)} %get-tuple-element.51, ...), kind=kOutput, calls=%fused_computation | convolution fusion | flops 20226375680 | bytes 32768000 | tf_op jit(solution)/shard_map/dot_general | solution.py:34
  811.0 5.0 fusion.127
  816.1 5.0 fusion.125
  821.1 23.6 %collective-permute-done.21 = bf16[256,2560]{1,0:T(8,128)(2,1)S(1)} collective-permute-done((bf16[256,2560]{1,0:T(8,128)(2,1)S(1)}, bf16[256,2560]{1,0:T(8,128)(2,1)S(1)}, u32[]{:S(2)}, u32[]{:S(2)}) %collective-permute-start.21) | collective-permute-done | bytes 1310752 | tf_op jit(solution)/shard_map/ppermute | solution.py:353
  847.0 25.3 %collective-permute-done.22 = bf16[256,2560]{1,0:T(8,128)(2,1)S(1)} collective-permute-done((bf16[256,2560]{1,0:T(8,128)(2,1)S(1)}, bf16[256,2560]{1,0:T(8,128)(2,1)S(1)}, u32[]{:S(2)}, u32[]{:S(2)}) %collective-permute-start.22) | collective-permute-done | bytes 1310752 | tf_op jit(solution)/shard_map/ppermute | solution.py:353
  873.8 4.5 fusion.121
  882.4 24.6 %all-reduce.12 = (f32[4,640]{1,0:T(4,128)}, f32[640]{0:T(1024)}, f32[640]{0:T(1024)}, f32[640]{0:T(1024)}, f32[640]{0:T(1024)}) all-reduce(f32[4,640]{1,0:T(4,128)S(1)} %slice.172, f32[640]{0:T(1024)S(1)} %get-tuple-element.36, f32[640]{0:T(1024)S(1)} %get-tuple-element.76, ...), channel_id=1, replica_groups=mesh['dp'=8,'tensor'=4] {'dp'}, use_global_device_ids=true, to_apply=%region_8.9 | all-reduce | flops 5120 | bytes 40960 | tf_op jit(solution)/shard_map/psum | solution.py:461
  907.0 2.9 fusion.69
  910.0 39.2 %all-reduce.11 = (f32[2560]{0:T(1024)}, f32[2560]{0:T(1024)}) all-reduce(f32[2560]{0:T(1024)S(1)} %get-tuple-element.33, f32[2560]{0:T(1024)S(1)} %get-tuple-element.31), channel_id=1, replica_groups=mesh['dp'=8,'tensor'=4] {'dp','tensor'}, use_global_device_ids=true, to_apply=%region_5.6 | all-reduce | flops 5120 | bytes 40960 | tf_op jit(solution)/shard_map/psum | solution.py:473
  949.2 4.9 fusion.71
  961.5 82.5 %reduce-scatter.9.cloned.1.call-done = bf16[320,3840]{1,0:T(8,128)(2,1)} async-done(((bf16[2560,3840]{1,0:T(8,128)(2,1)}), bf16[320,3840]{1,0:T(8,128)(2,1)}) %reduce-scatter.9.cloned.1.call-update) | async-done | bytes 2457616 | tf_op jit(solution)/shard_map/reduce_scatter | solution.py:437
  1044.0 4.3 fusion.168
  1048.3 61.2 %all-reduce.16.cloned.1.call-done = (f32[2,320,320]{2,1,0:T(8,128)}, f32[2,320,320]{2,1,0:T(8,128)}) async-done(((f32[2,320,320]{2,1,0:T(8,128)}, f32[2,320,320]{2,1,0:T(8,128)}), (f32[2,320,320]{2,1,0:T(8,128)}, f32[2,320,320]{2,1,0:T(8,128)})) %all-reduce.16.cloned.1.call-update) | async-done | bytes 1638416 | tf_op jit(solution)/shard_map/psum | solution.py:461
  (266 shorter events, 60.8 us)
Async XLA Ops:
  7.2 73.9 %all-gather.5.cloned.1.call-start = ((), (), s32[]{:S(2)}) async-start(), calls=%async_computation.4 | async-start | bytes 7372800 | tf_op jit(solution)/shard_map/all_gather | solution.py:371
  9.4 121.1 %all-gather.7.cloned.1.call-start = ((), (), s32[]{:S(2)}) async-start(), calls=%async_computation.5 | async-start | bytes 3686400 | tf_op jit(solution)/shard_map/all_gather | solution.py:372
  10.2 361.1 %all-gather.9.cloned.1.call-start = ((), (), s32[]{:S(2)}) async-start(), calls=%async_computation.6 | async-start | bytes 22118400 | tf_op jit(solution)/shard_map/all_gather | solution.py:373
  13.3 380.1 %all-gather.11.cloned.1.call-start = ((), (), s32[]{:S(2)}) async-start(), calls=%async_computation.7 | async-start | bytes 11059200 | tf_op jit(solution)/shard_map/all_gather | solution.py:374
  13.4 35.4 %copy-start.50 = (bf16[640]{0:T(1024)(128)(2,1)S(1)}, bf16[640]{0:T(1024)(128)(2,1)}, u32[]{:S(2)}) copy-start(bf16[640]{0:T(1024)(128)(2,1)} %param.25) | copy-start | bytes 3844
  13.4 35.4 %copy-start.47 = (bf16[4,640]{1,0:T(4,128)(2,1)S(1)}, bf16[4,640]{1,0:T(4,128)(2,1)}, u32[]{:S(2)}) copy-start(bf16[4,640]{1,0:T(4,128)(2,1)} %param.24) | copy-start | bytes 15364
  14.7 35.9 %copy-start.26 = (bf16[256,2560]{1,0:T(8,128)(2,1)}, bf16[256,2560]{1,0:T(8,128)(2,1)S(1)}, u32[]{:S(2)}) copy-start(bf16[256,2560]{1,0:T(8,128)(2,1)S(1)} %fusion.68) | copy-start | bytes 3932164
  14.8 34.0 %collective-permute-start = (bf16[256,2560]{1,0:T(8,128)(2,1)S(1)}, bf16[256,2560]{1,0:T(8,128)(2,1)}, u32[]{:S(2)}, u32[]{:S(2)}) collective-permute-start(bf16[256,2560]{1,0:T(8,128)(2,1)S(1)} %fusion.68), channel_id=1, source_target_pairs={{0,1},{1,2},{2,3},{3,0},{4,5},{5,6},{6,7},{7,4},{8,9},{9,10},{10,1... | collective-permute-start | bytes 3932168 | tf_op jit(solution)/shard_map/ppermute | solution.py:353
  17.9 936.2 %reduce-scatter.7.cloned.1.call-start = ((), (), s32[]{:S(2)}) async-start(), calls=%async_computation.9 | async-start | bytes 3686400 | tf_op jit(solution)/shard_map/reduce_scatter | solution.py:437
  18.4 99.8 %copy-start.5 = (f32[1,1280]{1,0:T(1,128)}, f32[1,1280]{1,0:T(1,128)S(1)}, u32[]{:S(2)}) copy-start(f32[1,1280]{1,0:T(1,128)S(1)} %maximum_convert_fusion.gate_b) | copy-start | bytes 15364
  48.8 32.1 %collective-permute-start.1 = (bf16[256,2560]{1,0:T(8,128)(2,1)}, bf16[256,2560]{1,0:T(8,128)(2,1)}, u32[]{:S(2)}, u32[]{:S(2)}) collective-permute-start(bf16[256,2560]{1,0:T(8,128)(2,1)} %collective-permute-done), channel_id=1, source_target_pairs={{0,1},{1,2},{2,3},{3,0},{4,5},{5,6},{6,7},{7,4},{8,9},{9,10},{10,1... | collective-permute-start | bytes 3932168 | tf_op jit(solution)/shard_map/ppermute | solution.py:353
  48.8 69.4 %copy-start.9 = (s32[4]{0:T(128)}, s32[4]{0:T(128)S(1)}, u32[]{:S(2)}) copy-start(s32[4]{0:T(128)S(1)} %compare_select_fusion.1.order) | copy-start | bytes 52
  48.8 69.4 %copy-start.7 = (f32[1,640]{1,0:T(1,128)}, f32[1,640]{1,0:T(1,128)S(1)}, u32[]{:S(2)}) copy-start(f32[1,640]{1,0:T(1,128)S(1)} %broadcast_in_dim.12.rate) | copy-start | bytes 7684
  80.8 31.5 %collective-permute-start.2 = (bf16[256,2560]{1,0:T(8,128)(2,1)}, bf16[256,2560]{1,0:T(8,128)(2,1)}, u32[]{:S(2)}, u32[]{:S(2)}) collective-permute-start(bf16[256,2560]{1,0:T(8,128)(2,1)} %collective-permute-done.1), channel_id=1, source_target_pairs={{0,1},{1,2},{2,3},{3,0},{4,5},{5,6},{6,7},{7,4},{8,9},{9,10},{10,1... | collective-permute-start | bytes 3932168 | tf_op jit(solution)/shard_map/ppermute | solution.py:353
  134.0 30.1 %collective-permute-start.3 = (bf16[256,2560]{1,0:T(8,128)(2,1)S(1)}, bf16[256,2560]{1,0:T(8,128)(2,1)S(1)}, u32[]{:S(2)}, u32[]{:S(2)}) collective-permute-start(bf16[256,2560]{1,0:T(8,128)(2,1)S(1)} %fusion.139), channel_id=1, source_target_pairs={{0,1},{1,2},{2,3},{3,0},{4,5},{5,6},{6,7},{7,4},{8,9},{9,10},{10,1... | collective-permute-start | bytes 3932168 | tf_op jit(solution)/shard_map/ppermute | solution.py:353
  164.4 29.2 %collective-permute-start.4 = (bf16[256,2560]{1,0:T(8,128)(2,1)S(1)}, bf16[256,2560]{1,0:T(8,128)(2,1)S(1)}, u32[]{:S(2)}, u32[]{:S(2)}) collective-permute-start(bf16[256,2560]{1,0:T(8,128)(2,1)S(1)} %add_convert_fusion.8), channel_id=1, source_target_pairs={{0,1},{1,2},{2,3},{3,0},{4,5},{5,6},{6,7},{7,4},{8,9},{9,10},{10,1... | collective-permute-start | bytes 3932168 | tf_op jit(solution)/shard_map/ppermute | solution.py:353
  165.7 28.9 %copy-start.46 = (bf16[2560]{0:T(1024)(128)(2,1)S(1)}, bf16[2560]{0:T(1024)(128)(2,1)}, u32[]{:S(2)}) copy-start(bf16[2560]{0:T(1024)(128)(2,1)} %param.32) | copy-start | bytes 15364
  193.9 28.9 %collective-permute-start.5 = (bf16[256,2560]{1,0:T(8,128)(2,1)S(1)}, bf16[256,2560]{1,0:T(8,128)(2,1)S(1)}, u32[]{:S(2)}, u32[]{:S(2)}) collective-permute-start(bf16[256,2560]{1,0:T(8,128)(2,1)S(1)} %add_convert_fusion.7), channel_id=1, source_target_pairs={{0,1},{1,2},{2,3},{3,0},{4,5},{5,6},{6,7},{7,4},{8,9},{9,10},{10,1... | collective-permute-start | bytes 3932168 | tf_op jit(solution)/shard_map/ppermute | solution.py:353
  194.5 29.1 %copy-start.32 = (f32[2560]{0:T(1024)}, f32[2560]{0:T(1024)S(1)}, u32[]{:S(2)}) copy-start(f32[2560]{0:T(1024)S(1)} %convert_element_type.205) | copy-start | bytes 30724
  194.5 28.3 %copy-start.14 = (bf16[256,2560]{1,0:T(8,128)(2,1)S(1)}, bf16[256,2560]{1,0:T(8,128)(2,1)}, u32[]{:S(2)}) copy-start(bf16[256,2560]{1,0:T(8,128)(2,1)} %param.18) | copy-start | bytes 3932164
  223.6 91.5 %copy-start.39 = (f32[256]{0:T(256)}, f32[256]{0:T(256)S(1)}, u32[]{:S(2)}) copy-start(f32[256]{0:T(256)S(1)} %get-tuple-element.48) | copy-start | bytes 3076
  223.6 63.4 %copy-start.37 = (f32[256]{0:T(256)}, f32[256]{0:T(256)S(1)}, u32[]{:S(2)}) copy-start(f32[256]{0:T(256)S(1)} %fusion.156) | copy-start | bytes 3076
  225.4 61.6 %copy-start.23 = (bf16[256,2560]{1,0:T(8,128)(2,1)}, bf16[256,2560]{1,0:T(8,128)(2,1)S(1)}, u32[]{:S(2)}) copy-start(bf16[256,2560]{1,0:T(8,128)(2,1)S(1)} %multiply_convert_fusion) | copy-start | bytes 3932164
  225.4 33.5 %collective-permute-start.6 = (bf16[256,2560]{1,0:T(8,128)(2,1)S(1)}, bf16[256,2560]{1,0:T(8,128)(2,1)S(1)}, u32[]{:S(2)}, u32[]{:S(2)}) collective-permute-start(bf16[256,2560]{1,0:T(8,128)(2,1)S(1)} %multiply_convert_fusion), channel_id=1, source_target_pairs={{0,1},{1,2},{2,3},{3,0},{4,5},{5,6},{6,7},{7,4},{8,9},{9,10},{10,1... | collective-permute-start | bytes 3932168 | tf_op jit(solution)/shard_map/ppermute | solution.py:353
  225.8 61.1 %collective-permute-start.12 = (bf16[256,2560]{1,0:T(8,128)(2,1)S(1)}, bf16[256,2560]{1,0:T(8,128)(2,1)S(1)}, u32[]{:S(2)}, u32[]{:S(2)}) collective-permute-start(bf16[256,2560]{1,0:T(8,128)(2,1)S(1)} %copy-done.19), channel_id=1, source_target_pairs={{0,1},{1,2},{2,3},{3,0},{4,5},{5,6},{6,7},{7,4},{8,9},{9,10},{10,1... | collective-permute-start | bytes 3932168 | tf_op jit(solution)/shard_map/ppermute | solution.py:353
  258.9 56.2 %copy-start.53 = (bf16[256,2560]{1,0:T(8,128)(2,1)}, bf16[256,2560]{1,0:T(8,128)(2,1)S(1)}, u32[]{:S(2)}) copy-start(bf16[256,2560]{1,0:T(8,128)(2,1)S(1)} %collective-permute-done.6) | copy-start | bytes 3932164
  258.9 56.2 %collective-permute-start.8 = (bf16[256,2560]{1,0:T(8,128)(2,1)S(1)}, bf16[256,2560]{1,0:T(8,128)(2,1)S(1)}, u32[]{:S(2)}, u32[]{:S(2)}) collective-permute-start(bf16[256,2560]{1,0:T(8,128)(2,1)S(1)} %collective-permute-done.6), channel_id=1, source_target_pairs={{0,1},{1,2},{2,3},{3,0},{4,5},{5,6},{6,7},{7,4},{8,9},{9,10},{10,1... | collective-permute-start | bytes 3932168 | tf_op jit(solution)/shard_map/ppermute | solution.py:353
  287.0 56.3 %copy-start.58 = (bf16[256,2560]{1,0:T(8,128)(2,1)}, bf16[256,2560]{1,0:T(8,128)(2,1)S(1)}, u32[]{:S(2)}) copy-start(bf16[256,2560]{1,0:T(8,128)(2,1)S(1)} %collective-permute-done.12) | copy-start | bytes 3932164
  287.0 56.3 %collective-permute-start.14 = (bf16[256,2560]{1,0:T(8,128)(2,1)S(1)}, bf16[256,2560]{1,0:T(8,128)(2,1)}, u32[]{:S(2)}, u32[]{:S(2)}) collective-permute-start(bf16[256,2560]{1,0:T(8,128)(2,1)S(1)} %collective-permute-done.12), channel_id=1, source_target_pairs={{0,1},{1,2},{2,3},{3,0},{4,5},{5,6},{6,7},{7,4},{8,9},{9,10},{10,1... | collective-permute-start | bytes 3932168 | tf_op jit(solution)/shard_map/ppermute | solution.py:353
  315.1 28.2 %copy-start.56 = (bf16[256,2560]{1,0:T(8,128)(2,1)}, bf16[256,2560]{1,0:T(8,128)(2,1)S(1)}, u32[]{:S(2)}) copy-start(bf16[256,2560]{1,0:T(8,128)(2,1)S(1)} %collective-permute-done.8) | copy-start | bytes 3932164
  315.1 56.3 %collective-permute-start.10 = (bf16[256,2560]{1,0:T(8,128)(2,1)S(1)}, bf16[256,2560]{1,0:T(8,128)(2,1)}, u32[]{:S(2)}, u32[]{:S(2)}) collective-permute-start(bf16[256,2560]{1,0:T(8,128)(2,1)S(1)} %collective-permute-done.8), channel_id=1, source_target_pairs={{0,1},{1,2},{2,3},{3,0},{4,5},{5,6},{6,7},{7,4},{8,9},{9,10},{10,1... | collective-permute-start | bytes 3932168 | tf_op jit(solution)/shard_map/ppermute | solution.py:353
  343.3 50.2 %collective-permute-start.16 = (bf16[256,2560]{1,0:T(8,128)(2,1)}, bf16[256,2560]{1,0:T(8,128)(2,1)}, u32[]{:S(2)}, u32[]{:S(2)}) collective-permute-start(bf16[256,2560]{1,0:T(8,128)(2,1)} %collective-permute-done.14), channel_id=1, source_target_pairs={{0,1},{1,2},{2,3},{3,0},{4,5},{5,6},{6,7},{7,4},{8,9},{9,10},{10,1... | collective-permute-start | bytes 3932168 | tf_op jit(solution)/shard_map/ppermute | solution.py:353
  403.6 116.6 %copy-start.66 = (bf16[256,1920]{1,0:T(8,128)(2,1)}, bf16[256,1920]{1,0:T(8,128)(2,1)S(1)}, u32[]{:S(2)}) copy-start(bf16[256,1920]{1,0:T(8,128)(2,1)S(1)} %get-tuple-element.60) | copy-start | bytes 2949124
  452.6 61.6 %collective-permute-start.7 = (bf16[256,2560]{1,0:T(8,128)(2,1)}, bf16[256,2560]{1,0:T(8,128)(2,1)}, u32[]{:S(2)}, u32[]{:S(2)}) collective-permute-start(bf16[256,2560]{1,0:T(8,128)(2,1)} %fusion.175), channel_id=1, source_target_pairs={{0,1},{1,2},{2,3},{3,0},{4,5},{5,6},{6,7},{7,4},{8,9},{9,10},{10,1... | collective-permute-start | bytes 3932168 | tf_op jit(solution)/shard_map/ppermute | solution.py:353
  452.6 59.2 %collective-permute-start.13 = (bf16[256,2560]{1,0:T(8,128)(2,1)}, bf16[256,2560]{1,0:T(8,128)(2,1)}, u32[]{:S(2)}, u32[]{:S(2)}) collective-permute-start(bf16[256,2560]{1,0:T(8,128)(2,1)} %fusion.102), channel_id=1, source_target_pairs={{0,1},{1,2},{2,3},{3,0},{4,5},{5,6},{6,7},{7,4},{8,9},{9,10},{10,1... | collective-permute-start | bytes 3932168 | tf_op jit(solution)/shard_map/ppermute | solution.py:353
  513.5 33.5 %collective-permute-start.15 = (bf16[256,2560]{1,0:T(8,128)(2,1)S(1)}, bf16[256,2560]{1,0:T(8,128)(2,1)S(1)}, u32[]{:S(2)}, u32[]{:S(2)}) collective-permute-start(bf16[256,2560]{1,0:T(8,128)(2,1)S(1)} %add_convert_fusion.3), channel_id=1, source_target_pairs={{0,1},{1,2},{2,3},{3,0},{4,5},{5,6},{6,7},{7,4},{8,9},{9,10},{10,1... | collective-permute-start | bytes 3932168 | tf_op jit(solution)/shard_map/ppermute | solution.py:353
  515.9 59.2 %collective-permute-start.9 = (bf16[256,2560]{1,0:T(8,128)(2,1)S(1)}, bf16[256,2560]{1,0:T(8,128)(2,1)S(1)}, u32[]{:S(2)}, u32[]{:S(2)}) collective-permute-start(bf16[256,2560]{1,0:T(8,128)(2,1)S(1)} %add_convert_fusion.6), channel_id=1, source_target_pairs={{0,1},{1,2},{2,3},{3,0},{4,5},{5,6},{6,7},{7,4},{8,9},{9,10},{10,1... | collective-permute-start | bytes 3932168 | tf_op jit(solution)/shard_map/ppermute | solution.py:353
  547.3 28.8 %copy-start.67 = (bf16[256,1920]{1,0:T(8,128)(2,1)S(1)}, bf16[256,1920]{1,0:T(8,128)(2,1)}, u32[]{:S(2)}) copy-start(bf16[256,1920]{1,0:T(8,128)(2,1)} %get-tuple-element.61) | copy-start | bytes 2949124
  547.3 55.8 %collective-permute-start.17 = (bf16[256,2560]{1,0:T(8,128)(2,1)S(1)}, bf16[256,2560]{1,0:T(8,128)(2,1)S(1)}, u32[]{:S(2)}, u32[]{:S(2)}) collective-permute-start(bf16[256,2560]{1,0:T(8,128)(2,1)S(1)} %add_convert_fusion.2), channel_id=1, source_target_pairs={{0,1},{1,2},{2,3},{3,0},{4,5},{5,6},{6,7},{7,4},{8,9},{9,10},{10,1... | collective-permute-start | bytes 3932168 | tf_op jit(solution)/shard_map/ppermute | solution.py:353
  575.4 49.0 %collective-permute-start.11 = (bf16[256,2560]{1,0:T(8,128)(2,1)S(1)}, bf16[256,2560]{1,0:T(8,128)(2,1)S(1)}, u32[]{:S(2)}, u32[]{:S(2)}) collective-permute-start(bf16[256,2560]{1,0:T(8,128)(2,1)S(1)} %add_convert_fusion.5), channel_id=1, source_target_pairs={{0,1},{1,2},{2,3},{3,0},{4,5},{5,6},{6,7},{7,4},{8,9},{9,10},{10,1... | collective-permute-start | bytes 3932168 | tf_op jit(solution)/shard_map/ppermute | solution.py:353
  576.1 27.1 %copy-start.12 = (f32[256,2560]{1,0:T(8,128)S(1)}, f32[256,2560]{1,0:T(8,128)}, u32[]{:S(2)}) copy-start(f32[256,2560]{1,0:T(8,128)} %copy-done.11) | copy-start | bytes 7864324
  576.1 27.1 %copy-start.33 = (f32[2560]{0:T(1024)S(1)}, f32[2560]{0:T(1024)}, u32[]{:S(2)}) copy-start(f32[2560]{0:T(1024)} %copy-done.32) | copy-start | bytes 30724
  576.1 27.1 %copy-start.38 = (f32[256]{0:T(256)S(1)}, f32[256]{0:T(256)}, u32[]{:S(2)}) copy-start(f32[256]{0:T(256)} %copy-done.37) | copy-start | bytes 3076
  581.8 22.3 %copy-start.40 = (f32[256]{0:T(256)S(1)}, f32[256]{0:T(256)}, u32[]{:S(2)}) copy-start(f32[256]{0:T(256)} %copy-done.39) | copy-start | bytes 3076
  581.8 42.6 %copy-start.21 = (bf16[256,2560]{1,0:T(8,128)(2,1)S(1)}, bf16[256,2560]{1,0:T(8,128)(2,1)}, u32[]{:S(2)}) copy-start(bf16[256,2560]{1,0:T(8,128)(2,1)} %param.20) | copy-start | bytes 3932164
  604.2 106.8 %copy-start.2 = (bf16[4,256,640]{2,1,0:T(8,128)(2,1)S(1)}, bf16[4,256,640]{2,1,0:T(8,128)(2,1)}, u32[]{:S(2)}) copy-start(bf16[4,256,640]{2,1,0:T(8,128)(2,1)} %copy-done) | copy-start | bytes 3932164
  628.0 81.9 %copy-start.22 = (bf16[256,2560]{1,0:T(8,128)(2,1)}, bf16[256,2560]{1,0:T(8,128)(2,1)S(1)}, u32[]{:S(2)}) copy-start(bf16[256,2560]{1,0:T(8,128)(2,1)S(1)} %get-tuple-element.46) | copy-start | bytes 3932164
  628.0 28.9 %collective-permute-start.18 = (bf16[256,2560]{1,0:T(8,128)(2,1)S(1)}, bf16[256,2560]{1,0:T(8,128)(2,1)S(1)}, u32[]{:S(2)}, u32[]{:S(2)}) collective-permute-start(bf16[256,2560]{1,0:T(8,128)(2,1)S(1)} %get-tuple-element.46), channel_id=1, source_target_pairs={{0,1},{1,2},{2,3},{3,0},{4,5},{5,6},{6,7},{7,4},{8,9},{9,10},{10,1... | collective-permute-start | bytes 3932168 | tf_op jit(solution)/shard_map/ppermute | solution.py:353
  656.9 53.0 %copy-start.60 = (bf16[256,2560]{1,0:T(8,128)(2,1)}, bf16[256,2560]{1,0:T(8,128)(2,1)S(1)}, u32[]{:S(2)}) copy-start(bf16[256,2560]{1,0:T(8,128)(2,1)S(1)} %collective-permute-done.18) | copy-start | bytes 3932164
  656.9 28.9 %collective-permute-start.19 = (bf16[256,2560]{1,0:T(8,128)(2,1)S(1)}, bf16[256,2560]{1,0:T(8,128)(2,1)S(1)}, u32[]{:S(2)}, u32[]{:S(2)}) collective-permute-start(bf16[256,2560]{1,0:T(8,128)(2,1)S(1)} %collective-permute-done.18), channel_id=1, source_target_pairs={{0,1},{1,2},{2,3},{3,0},{4,5},{5,6},{6,7},{7,4},{8,9},{9,10},{10,1... | collective-permute-start | bytes 3932168 | tf_op jit(solution)/shard_map/ppermute | solution.py:353
  685.9 24.0 %copy-start.62 = (bf16[256,2560]{1,0:T(8,128)(2,1)}, bf16[256,2560]{1,0:T(8,128)(2,1)S(1)}, u32[]{:S(2)}) copy-start(bf16[256,2560]{1,0:T(8,128)(2,1)S(1)} %collective-permute-done.19) | copy-start | bytes 3932164
  685.9 24.0 %collective-permute-start.20 = (bf16[256,2560]{1,0:T(8,128)(2,1)S(1)}, bf16[256,2560]{1,0:T(8,128)(2,1)S(1)}, u32[]{:S(2)}, u32[]{:S(2)}) collective-permute-start(bf16[256,2560]{1,0:T(8,128)(2,1)S(1)} %collective-permute-done.19), channel_id=1, source_target_pairs={{0,1},{1,2},{2,3},{3,0},{4,5},{5,6},{6,7},{7,4},{8,9},{9,10},{10,1... | collective-permute-start | bytes 3932168 | tf_op jit(solution)/shard_map/ppermute | solution.py:353
  717.0 239.1 %reduce-scatter.11.cloned.1.call-start = ((), (), s32[]{:S(2)}) async-start(), calls=%async_computation.11 | async-start | bytes 11059200 | tf_op jit(solution)/shard_map/reduce_scatter | solution.py:437
  733.5 225.4 %reduce-scatter.5.cloned.1.call-start = ((), (), s32[]{:S(2)}) async-start(), calls=%async_computation.8 | async-start | bytes 7372800 | tf_op jit(solution)/shard_map/reduce_scatter | solution.py:437
  776.8 267.2 %reduce-scatter.9.cloned.1.call-start = ((), (), s32[]{:S(2)}) async-start(), calls=%async_computation.10 | async-start | bytes 22118400 | tf_op jit(solution)/shard_map/reduce_scatter | solution.py:437
  809.3 300.2 %all-reduce.16.cloned.1.call-start = ((), (), s32[]{:S(2)}) async-start(), calls=%async_computation.12 | async-start | bytes 3932160 | tf_op jit(solution)/shard_map/psum | solution.py:461
  811.0 34.0 %slice-start.3 = ((s8[6553600]{0:T(1024)(128)(4,1)}), s8[4194304]{0:T(1024)(128)(4,1)S(1)}, s32[]{:S(2)}) async-start(s8[6553600]{0:T(1024)(128)(4,1)} %bitcast.141), calls=%async_computation.16 | async-start | bytes 8388608
  816.0 29.0 %slice-start.4 = ((s8[6553600]{0:T(1024)(128)(4,1)}), s8[2359296]{0:T(1024)(128)(4,1)S(1)}, s32[]{:S(2)}) async-start(s8[6553600]{0:T(1024)(128)(4,1)} %bitcast.141), calls=%async_computation.17 | async-start | bytes 4718592
  816.0 28.6 %collective-permute-start.21 = (bf16[256,2560]{1,0:T(8,128)(2,1)S(1)}, bf16[256,2560]{1,0:T(8,128)(2,1)S(1)}, u32[]{:S(2)}, u32[]{:S(2)}) collective-permute-start(bf16[256,2560]{1,0:T(8,128)(2,1)S(1)} %fusion.127), channel_id=1, source_target_pairs={{0,1},{1,2},{2,3},{3,0},{4,5},{5,6},{6,7},{7,4},{8,9},{9,10},{10,1... | collective-permute-start | bytes 3932168 | tf_op jit(solution)/shard_map/ppermute | solution.py:353
  845.0 27.3 %collective-permute-start.22 = (bf16[256,2560]{1,0:T(8,128)(2,1)S(1)}, bf16[256,2560]{1,0:T(8,128)(2,1)S(1)}, u32[]{:S(2)}, u32[]{:S(2)}) collective-permute-start(bf16[256,2560]{1,0:T(8,128)(2,1)S(1)} %add_convert_fusion.1), channel_id=1, source_target_pairs={{0,1},{1,2},{2,3},{3,0},{4,5},{5,6},{6,7},{7,4},{8,9},{9,10},{10,1... | collective-permute-start | bytes 3932168 | tf_op jit(solution)/shard_map/ppermute | solution.py:353
  873.6 33.4 %collective-permute-start.23 = (bf16[256,2560]{1,0:T(8,128)(2,1)}, bf16[256,2560]{1,0:T(8,128)(2,1)S(1)}, u32[]{:S(2)}, u32[]{:S(2)}) collective-permute-start(bf16[256,2560]{1,0:T(8,128)(2,1)} %add_convert_fusion), channel_id=1, source_target_pairs={{0,1},{1,2},{2,3},{3,0},{4,5},{5,6},{6,7},{7,4},{8,9},{9,10},{10,1... | collective-permute-start | bytes 3932168 | tf_op jit(solution)/shard_map/ppermute | solution.py:353
  880.3 26.8 %copy-start.15 = (bf16[256,2560]{1,0:T(8,128)(2,1)S(1)}, bf16[256,2560]{1,0:T(8,128)(2,1)}, u32[]{:S(2)}) copy-start(bf16[256,2560]{1,0:T(8,128)(2,1)} %param.18) | copy-start | bytes 3932164
  880.3 26.8 %copy-start.31 = (f32[2560]{0:T(1024)S(1)}, f32[2560]{0:T(1024)}, u32[]{:S(2)}) copy-start(f32[2560]{0:T(1024)} %copy-done.30) | copy-start | bytes 30724
  880.3 26.7 %copy-start.36 = (f32[256]{0:T(256)S(1)}, f32[256]{0:T(256)}, u32[]{:S(2)}) copy-start(f32[256]{0:T(256)} %copy-done.35) | copy-start | bytes 3076
  (46 other events, 230.7 us)
Sparse Core Ops, SparseCore 0:
  10.5 49.2 all-gather.4
  61.6 32.7 all-gather.6
  96.8 101.9 all-gather.8
  200.5 60.3 all-gather.10
  717.1 44.3 reduce-scatter.6
  764.9 78.6 reduce-scatter.10
  847.0 63.2 reduce-scatter.4
  914.0 129.9 reduce-scatter.8
  1048.5 60.9 all-reduce.15
